TPU v7x, 512 devices: a whole 4x8x8 slice. The times are simulated.
512 devices in a mesh: batch: 32 (over z_lo, y, core), gy: 4 (over z_hi), gx: 4 (over x).
Axes of the slice: x: 4, y: 8, z: 8 (z_hi: 4, z_lo: 2; z = z_hi * 2 + z_lo), core: 2. Of those that a mesh axis runs over, the one named last changes fastest.
Arguments:
- x_fine: bfloat16 [32, 32, 128, 256], P('batch', 'gy', 'gx'), may hold values from -6 to 6
- dy_fine: bfloat16 [32, 32, 128, 256], P('batch', 'gy', 'gx'), may hold values from -6 to 6
- x_coarse: bfloat16 [32, 16, 16, 1024], P('batch', 'gy', 'gx'), may hold values from -6 to 6
- dy_coarse: bfloat16 [32, 16, 16, 1024], P('batch', 'gy', 'gx'), may hold values from -6 to 6
- timestep: int32 [32], P('batch'), may hold values from 0 to 999
- fine_gain: float32 [256], replicated, may hold values from 0.5 to 2.5, as said below
- coarse_gain: float32 [1024], replicated, may hold values from 0.5 to 2.5, as said below
- fine_qkv: bfloat16 [256, 768], replicated, may hold values from -0.375 to 0.375
- fine_out: bfloat16 [256, 256], replicated, may hold values from -0.375 to 0.375
- coarse_qkv: bfloat16 [3, 1024, 1024], P(None, ('gy', 'gx')), may hold values from -0.1875 to 0.1875
- coarse_out: bfloat16 [1024, 1024], P(('gy', 'gx')), may hold values from -0.1875 to 0.1875
Outputs:
- dx_fine: bfloat16 [32, 32, 128, 256], P('batch', 'gy', 'gx')
- dx_coarse: bfloat16 [32, 16, 16, 1024], P('batch', 'gy', 'gx')
- grad_fine_qkv: bfloat16 [256, 768], replicated
- grad_fine_out: bfloat16 [256, 256], replicated
- grad_coarse_qkv: bfloat16 [3, 1024, 1024], P(None, ('gy', 'gx'))
- grad_coarse_out: bfloat16 [1024, 1024], P(('gy', 'gx'))
Inputs may be any that keep to these rules, and one draw needn't show every extreme that they name: `fine_gain`: the norm gains are positive. `coarse_gain`: the norm gains are positive.
All inputs are finite; a program needn't handle non-finite values.
Results may differ from a plain program's by a relative error of at most 0.017.
The roundings to bfloat16 on the way count: a program that leaves them out, or rounds other values in their place, can miss the bound.
Values may be sent and summed in bfloat16 or wider, within the bound.
A program may use at most 64 MiB of HBM per device.

v0:
```python
import math

import jax
import jax.numpy as jnp
from jax import lax
from jax.sharding import PartitionSpec as P

D_F = 256
H_F = 4
D_C = 1024
HD = 64
RAD = 3


eps = 1e-06
log_span = math.log(1000.0)
block_side = 8


def padded_2(array, sides, width):
    for axis, dim in sides:
        peers, length = (lax.axis_size(axis), array.shape[dim])
        up = [(i, (i + 1) % peers) for i in range(peers - 1)]
        down = [(j, i) for i, j in up]
        last = lax.slice_in_dim(array, length - width, length, axis=dim)
        leading = lax.slice_in_dim(array, 0, width, axis=dim)
        before = lax.ppermute(last, axis, up)
        after = lax.ppermute(leading, axis, down)
        array = jnp.concatenate([before, array, after], axis=dim)
    return array


def shifted(value, axis, steps):
    count = lax.axis_size(axis)
    leading, last = (max(0, -steps), min(count, count - steps))
    return lax.ppermute(value, axis, [(source, source + steps) for source in range(leading, last)])


def contract(pattern, first_op, second_op):
    return jnp.einsum(pattern, first_op, second_op, preferred_element_type=jnp.float32)


def score_scale():
    return 1.0 / math.sqrt(HD)


def time_gain(gains, step_value):
    channels = gains.shape[0]
    frequency = jnp.exp(-log_span * jnp.arange(channels, dtype=jnp.float32) / channels)
    return gains * (1.0 + 0.5 * jnp.cos(step_value.astype(jnp.float32) * frequency))


def norm_forward(source, factor):
    floats = source.astype(jnp.float32)
    inverse = lax.rsqrt(jnp.mean(floats * floats, axis=-1, keepdims=True) + eps)
    return ((floats * inverse * factor).astype(jnp.bfloat16), inverse)


def norm_backward(source, inverse, factor, upstream):
    floats = source.astype(jnp.float32)
    scaled = upstream * factor
    middle = jnp.mean(floats * scaled, axis=-1, keepdims=True)
    return (inverse * scaled - floats * inverse * inverse * inverse * middle).astype(jnp.bfloat16)


def to_tiles(planar):
    height, breadth, channels = planar.shape
    pieces = planar.reshape(
        height // block_side, block_side, breadth // block_side, block_side, channels
    )
    return pieces.transpose(0, 2, 1, 3, 4).reshape(-1, block_side * block_side, channels)


def from_tiles(blocks, height, breadth):
    channels = blocks.shape[-1]
    pieces = blocks.reshape(
        height // block_side, breadth // block_side, block_side, block_side, channels
    )
    return pieces.transpose(0, 2, 1, 3, 4).reshape(height, breadth, channels)


def windows(padded, height, breadth):
    extent = block_side + 2 * RAD
    block_rows = height // block_side
    across = breadth // block_side
    channels = padded.shape[-1]
    widened = jnp.pad(
        padded,
        (
            (0, (block_rows + 1) * block_side - padded.shape[0]),
            (0, (across + 1) * block_side - padded.shape[1]),
            (0, 0),
        ),
    )
    blocks_grid = widened.reshape(
        block_rows + 1, block_side, across + 1, block_side, channels
    ).transpose(0, 2, 1, 3, 4)
    upper_pair = jnp.concatenate([blocks_grid[:-1, :-1], blocks_grid[:-1, 1:]], axis=3)
    lower_pair = jnp.concatenate([blocks_grid[1:, :-1], blocks_grid[1:, 1:]], axis=3)
    square = jnp.concatenate([upper_pair, lower_pair], axis=2)
    return square[:, :, :extent, :extent].reshape(block_rows * across, extent * extent, channels)


def intersection_add(windowed, height, breadth):
    extent = block_side + 2 * RAD
    block_rows = height // block_side
    across = breadth // block_side
    channels = windowed.shape[-1]
    layout = windowed.reshape(block_rows, across, extent, extent, channels)
    layout = jnp.pad(
        layout, ((0, 0), (0, 0), (0, 2 * block_side - extent), (0, 2 * block_side - extent), (0, 0))
    )
    summed = jnp.zeros((block_rows + 1, across + 1, block_side, block_side, channels), jnp.float32)
    for row_half in range(2):
        for col_half in range(2):
            quarter = layout[
                :,
                :,
                row_half * block_side : (row_half + 1) * block_side,
                col_half * block_side : (col_half + 1) * block_side,
            ]
            summed = summed + jnp.pad(
                quarter,
                ((row_half, 1 - row_half), (col_half, 1 - col_half), (0, 0), (0, 0), (0, 0)),
            )
    merged = summed.transpose(0, 2, 1, 3, 4).reshape(
        (block_rows + 1) * block_side, (across + 1) * block_side, channels
    )
    return merged[: height + 2 * RAD, : breadth + 2 * RAD]


def pair_mask():
    extent = block_side + 2 * RAD
    inner_pos = jnp.arange(block_side * block_side)
    outer_pos = jnp.arange(extent * extent)
    row_gap = outer_pos[None, :] // extent - inner_pos[:, None] // block_side
    col_gap = outer_pos[None, :] % extent - inner_pos[:, None] % block_side
    return (row_gap >= 0) & (row_gap <= 2 * RAD) & (col_gap >= 0) & (col_gap <= 2 * RAD)


def fine_forward(queries, key_values, valid_pad):
    height, breadth, channels = queries.shape
    query_blocks = to_tiles(queries)
    block_count = query_blocks.shape[0]
    query_heads = query_blocks.reshape(block_count, -1, H_F, HD)
    key_windows = windows(key_values, height, breadth)
    key_heads = key_windows[..., :channels].reshape(block_count, -1, H_F, HD)
    value_heads = key_windows[..., channels:].reshape(block_count, -1, H_F, HD)
    allowed = (
        pair_mask()[None, None]
        & windows(valid_pad[..., None], height, breadth)[:, None, None, :, 0]
    )
    scores = contract("bqhe,bkhe->bhqk", query_heads, key_heads) * score_scale()
    scores = jnp.where(allowed, scores, -1e30)
    peak = jnp.max(scores, axis=-1, keepdims=True)
    log_total = peak + jnp.log(jnp.sum(jnp.exp(scores - peak), axis=-1, keepdims=True))
    shares = jnp.where(allowed, jnp.exp(scores - log_total), 0.0)
    weights = shares.astype(jnp.bfloat16)
    mixed = contract("bhqk,bkhe->bqhe", weights, value_heads).astype(jnp.bfloat16)
    attended = from_tiles(mixed.reshape(block_count, -1, channels), height, breadth)
    return (attended, query_heads, key_heads, value_heads, shares, weights, log_total)


def fine_query_backward(upstream, query_heads, key_heads, value_heads, shares, height, breadth):
    block_count = query_heads.shape[0]
    upward_heads = to_tiles(upstream).reshape(block_count, -1, H_F, HD)
    products = contract("bqhe,bkhe->bhqk", upward_heads, value_heads)
    centre = jnp.sum(shares * products, axis=-1, keepdims=True)
    slopes = (shares * (products - centre)).astype(jnp.bfloat16)
    grad_query = contract("bhqk,bkhe->bqhe", slopes, key_heads) * score_scale()
    grad_query = from_tiles(grad_query.reshape(block_count, -1, H_F * HD), height, breadth)
    return (grad_query, upward_heads, slopes, centre)


def key_grads_windows(slopes, weights, query_heads, upward_heads):
    block_count = query_heads.shape[0]
    grad_key = contract("bhqk,bqhe->bkhe", slopes, query_heads).reshape(block_count, -1, D_F)
    grad_value = contract("bhqk,bqhe->bkhe", weights, upward_heads).reshape(block_count, -1, D_F)
    return jnp.concatenate([grad_key, grad_value], axis=-1)


def local(
    x_fine,
    dy_fine,
    x_coarse,
    dy_coarse,
    timestep,
    fine_gain,
    coarse_gain,
    fine_qkv,
    fine_out,
    coarse_qkv,
    coarse_out,
):
    step_value = timestep[0]
    picture = x_fine[0]
    height, breadth = (picture.shape[0], picture.shape[1])
    factor = time_gain(fine_gain, step_value)
    normed, inverse = norm_forward(picture, factor)
    flat_normed = normed.reshape(-1, D_F)
    projected = (
        jnp.dot(flat_normed, fine_qkv, preferred_element_type=jnp.float32)
        .astype(jnp.bfloat16)
        .reshape(height, breadth, 3 * D_F)
    )
    queries = projected[..., :D_F]
    key_values = projected[..., D_F:]
    kv_pad = padded_2(key_values[None], (("gy", 1), ("gx", 2)), RAD)[0]
    row_first = lax.axis_index("gy") * height - RAD
    col_first = lax.axis_index("gx") * breadth - RAD
    pad_rows = row_first + jnp.arange(height + 2 * RAD, dtype=jnp.int32)
    pad_cols = col_first + jnp.arange(breadth + 2 * RAD, dtype=jnp.int32)
    rows_inside = (pad_rows >= 0) & (pad_rows < height * lax.axis_size("gy"))
    cols_inside = (pad_cols >= 0) & (pad_cols < breadth * lax.axis_size("gx"))
    valid_pad = rows_inside[:, None] & cols_inside[None, :]
    attended, query_heads, key_heads, value_heads, shares, weights, log_total = fine_forward(
        queries, kv_pad, valid_pad
    )
    flat_cot = dy_fine[0].reshape(-1, D_F)
    grad_out_local = lax.dot_general(
        attended.reshape(-1, D_F),
        flat_cot,
        (((0,), (0,)), ((), ())),
        preferred_element_type=jnp.float32,
    )
    upstream = (
        lax.dot_general(
            flat_cot, fine_out, (((1,), (1,)), ((), ())), preferred_element_type=jnp.float32
        )
        .astype(jnp.bfloat16)
        .reshape(height, breadth, D_F)
    )
    grad_query, upward_heads, slopes, centre = fine_query_backward(
        upstream, query_heads, key_heads, value_heads, shares, height, breadth
    )
    summed = intersection_add(
        key_grads_windows(slopes, weights, query_heads, upward_heads), height, breadth
    )
    from_left = shifted(summed[:, breadth + RAD :], "gx", 1)
    from_right = shifted(summed[:, :RAD], "gx", -1)
    middle = summed[:, RAD : breadth + RAD]
    middle = middle.at[:, :RAD].add(from_left)
    middle = middle.at[:, breadth - RAD :].add(from_right)
    from_above = shifted(middle[height + RAD :], "gy", 1)
    from_below = shifted(middle[:RAD], "gy", -1)
    key_grads = middle[RAD : height + RAD]
    key_grads = key_grads.at[:RAD].add(from_above)
    key_grads = key_grads.at[height - RAD :].add(from_below)
    grad_proj = (
        jnp.concatenate(
            [grad_query, key_grads[..., :D_F] * score_scale(), key_grads[..., D_F:]], axis=-1
        )
        .astype(jnp.bfloat16)
        .reshape(-1, 3 * D_F)
    )
    grad_qkv_local = lax.dot_general(
        flat_normed, grad_proj, (((0,), (0,)), ((), ())), preferred_element_type=jnp.float32
    )
    down_grad = lax.dot_general(
        grad_proj, fine_qkv, (((1,), (1,)), ((), ())), preferred_element_type=jnp.float32
    ).reshape(height, breadth, D_F)
    dx_picture = norm_backward(picture, inverse, factor, down_grad)
    coarse_tokens = x_coarse[0].reshape(-1, D_C)
    coarse_factor = time_gain(coarse_gain, step_value)
    coarse_normed, coarse_inverse = norm_forward(coarse_tokens, coarse_factor)
    coarse_cot = dy_coarse[0].reshape(-1, D_C)
    all_normed = lax.all_gather(coarse_normed, ("gy", "gx"), axis=0, tiled=True)
    coarse_proj = contract("td,khd->kth", all_normed, coarse_qkv).astype(jnp.bfloat16)
    head_queries, head_keys, head_values = (coarse_proj[0], coarse_proj[1], coarse_proj[2])
    coarse_scores = contract("te,se->ts", head_queries, head_keys) * score_scale()
    coarse_peak = jnp.max(coarse_scores, axis=-1, keepdims=True)
    coarse_log = coarse_peak + jnp.log(
        jnp.sum(jnp.exp(coarse_scores - coarse_peak), axis=-1, keepdims=True)
    )
    coarse_shares = jnp.exp(coarse_scores - coarse_log)
    coarse_weights = coarse_shares.astype(jnp.bfloat16)
    head_mixed = contract("ts,se->te", coarse_weights, head_values).astype(jnp.bfloat16)
    all_cot = lax.all_gather(coarse_cot, ("gy", "gx"), axis=0, tiled=True)
    head_upstream = contract("td,ed->te", all_cot, coarse_out).astype(jnp.bfloat16)
    coarse_out_local = contract("te,td->ed", head_mixed, all_cot)
    coarse_products = contract("te,se->ts", head_upstream, head_values)
    coarse_centre = jnp.sum(coarse_shares * coarse_products, axis=-1, keepdims=True)
    coarse_slopes = (coarse_shares * (coarse_products - coarse_centre)).astype(jnp.bfloat16)
    head_grad_query = (contract("ts,se->te", coarse_slopes, head_keys) * score_scale()).astype(
        jnp.bfloat16
    )
    head_grad_key = (contract("ts,te->se", coarse_slopes, head_queries) * score_scale()).astype(
        jnp.bfloat16
    )
    head_grad_value = contract("ts,te->se", coarse_weights, head_upstream).astype(jnp.bfloat16)
    stacked = jnp.stack([head_grad_query, head_grad_key, head_grad_value])
    coarse_qkv_local = contract("kte,td->ked", stacked, all_normed)
    head_part = contract("kte,ked->td", stacked, coarse_qkv)
    coarse_down = lax.psum_scatter(
        head_part.astype(jnp.bfloat16), ("gy", "gx"), scatter_dimension=0, tiled=True
    ).astype(jnp.float32)
    dx_coarse_tok = norm_backward(coarse_tokens, coarse_inverse, coarse_factor, coarse_down)
    fine_qkv_sum, fine_out_sum = lax.psum((grad_qkv_local, grad_out_local), ("batch", "gy", "gx"))
    coarse_qkv_sum, coarse_out_sum = lax.psum((coarse_qkv_local, coarse_out_local), "batch")
    return (
        dx_picture[None],
        dx_coarse_tok.reshape(x_coarse.shape),
        fine_qkv_sum.astype(jnp.bfloat16),
        fine_out_sum.astype(jnp.bfloat16),
        coarse_qkv_sum.astype(jnp.bfloat16),
        coarse_out_sum.astype(jnp.bfloat16),
    )


def solution(mesh):
    placed = (
        P("batch", "gy", "gx", None),
        P("batch", "gy", "gx", None),
        P("batch", "gy", "gx", None),
        P("batch", "gy", "gx", None),
        P("batch"),
        P(),
        P(),
        P(),
        P(),
        P(None, ("gy", "gx"), None),
        P(("gy", "gx"), None),
    )
    return jax.shard_map(
        local,
        mesh=mesh,
        in_specs=placed,
        out_specs=(
            P("batch", "gy", "gx", None),
            P("batch", "gy", "gx", None),
            P(),
            P(),
            P(None, ("gy", "gx"), None),
            P(("gy", "gx"), None),
        ),
        check_vma=False,
    )
```

profile of v0, /device:TPU:1, one launch (start us, length us, event | category | flops | bytes accessed | tf_op | source)
XLA Modules:
  0.0 400.2 jit_solution(13088266657257998717)
XLA Ops:
  7.9 1.0 fusion.28
  9.1 0.5 copy-done.14
  9.6 0.7 add_multiply_fusion.1
  10.3 1.0 fusion.20
  11.3 1.3 convolution_convert_fusion
  12.7 6.8 %collective-permute-start = (bf16[1,3,32,512]{3,2,1,0:T(8,128)(2,1)S(1)}, bf16[1,3,32,512]{3,2,1,0:T(8,128)(2,1)S(1)}, u32[]{:S(2)}, u32[]{:S(2)}) collective-permute-start(bf16[1,3,32,512]{3,2,1,0:T(8,128)(2,1)S(1)} %get-tuple-element.74), channel_id=1, source_target_pairs={{0,4},{4,8},{8,12},{1,5},{5,9},{9,13},{2,6},{6,10},{10,14},{3,7},{... | collective-permute-start | bytes 294920 | tf_op jit(solution)/shard_map/ppermute | solution.py:27
  19.4 1.3 collective-permute-start.1
  21.1 44.2 %all_gather.6 = bf16[256,1024]{1,0:T(8,128)(2,1)S(1)} all-gather(bf16[16,1024]{1,0:T(8,128)(2,1)S(1)} %multiply_convert_fusion.2), channel_id=1, replica_groups=mesh['batch'=32,'gy'=4,'gx'=4] {'gy','gx'}, dimensions={0}, use_global_device_ids=true | all-gather | bytes 557056 | tf_op jit(solution)/shard_map/all_gather | solution.py:267
  65.3 0.3 fusion.5
  65.6 0.3 fusion.63
  66.0 34.0 %all_gather.7 = bf16[256,1024]{1,0:T(8,128)(2,1)S(1)} all-gather(bf16[16,1024]{1,0:T(8,128)(2,1)S(1)} %reshape_squeeze.8), channel_id=1, replica_groups=mesh['batch'=32,'gy'=4,'gx'=4] {'gy','gx'}, dimensions={0}, use_global_device_ids=true | all-gather | bytes 557056 | tf_op jit(solution)/shard_map/all_gather | solution.py:278
  100.0 0.3 convolution_convert_fusion.6
  100.5 0.3 multiply_reduce_fusion.1
  101.2 1.1 fusion.1
  102.4 0.4 fusion.9
  102.8 0.3 fusion.14
  103.3 0.2 convolution_convert_fusion.2
  103.5 131.1 %all-reduce.11 = (bf16[3,64,1024]{2,1,0:T(8,128)(2,1)}, bf16[64,1024]{1,0:T(8,128)(2,1)}) all-reduce(f32[3,64,1024]{2,1,0:T(8,128)S(1)} %fusion.14, f32[64,1024]{1,0:T(8,128)S(1)} %fusion.9), channel_id=1, replica_groups=mesh['batch'=32,'gy'=4,'gx'=4] {'batch'}, use_global_device_ids=true, to_apply=%region_13.14 | all-reduce | flops 262144 | bytes 1572864 | tf_op jit(solution)/shard_map/psum | solution.py:299
  235.0 2.2 collective-permute-start.2
  237.2 1.5 collective-permute-start.3
  239.5 2.6 collective-permute-done.3
  242.1 0.2 maximum_bitcast_fusion
  242.6 0.7 copy.38
  243.2 0.3 fusion.58
  243.5 0.3 copy.39
  243.8 0.3 copy.44
  244.2 0.4 fusion.62
  244.6 0.4 exponential_reduce_fusion
  245.0 0.4 fusion.3
  245.5 0.6 multiply_reduce_fusion
  246.1 0.4 convolution_bitcast_fusion.1
  246.5 0.4 multiply_convert_fusion
  246.8 1.0 fusion.4
  247.8 1.3 convolution_bitcast_fusion.2
  249.3 0.2 reshape_reshape.23
  249.5 2.0 copy.49
  251.6 1.9 concatenate.57
  253.5 1.1 copy.51
  254.6 1.9 concatenate.58
  256.7 0.9 copy-done.2
  257.8 0.4 fusion.55
  258.3 0.4 add_bitcast_fusion
  258.7 1.0 copy.52
  259.8 0.7 fusion.56
  260.5 2.6 collective-permute-start.4
  263.0 0.9 fusion.64
  264.3 0.2 reshape_reshape.22
  264.5 1.3 collective-permute-start.5
  265.8 0.9 slice_add_fusion.3
  266.8 0.4 scatter-add.14
  267.2 2.9 collective-permute-done.5
  270.1 0.3 scatter-add.15
  270.5 1.4 collective-permute-start.6
  272.0 1.3 collective-permute-start.7
  273.3 1.2 collective-permute-done.6
  274.6 6.9 %collective-permute-done.7 = f32[3,32,512]{2,1,0:T(8,128)S(1)} collective-permute-done((f32[3,32,512]{2,1,0:T(8,128)S(1)}, f32[3,32,512]{2,1,0:T(8,128)S(1)}, u32[]{:S(2)}, u32[]{:S(2)}) %collective-permute-start.7) | collective-permute-done | bytes 196640 | tf_op jit(solution)/shard_map/ppermute | solution.py:36
  281.7 0.4 convolution_bitcast_fusion.3
  282.1 0.5 copy-done.8
  282.6 0.4 fusion.29
  283.0 0.8 fusion.34
  283.8 107.2 %all-reduce.12 = (bf16[256,768]{1,0:T(8,128)(2,1)}, bf16[256,256]{1,0:T(8,128)(2,1)}) all-reduce(f32[256,768]{1,0:T(8,128)S(1)} %convolution_bitcast_fusion.3, f32[256,256]{1,0:T(8,128)S(1)} %copy-done.5), channel_id=1, replica_groups=mesh['batch'=32,'gy'=4,'gx'=4] {'batch','gy','gx'}, use_global_device_ids=true, to_apply=%region_11.12 | all-reduce | flops 262144 | bytes 1572864 | tf_op jit(solution)/shard_map/psum | solution.py:298
  391.0 0.9 multiply_reduce_fusion.2
  391.9 0.8 subtract_convert_fusion
  392.7 0.6 reshape.470
  (106 shorter events, 4.0 us)
Async XLA Ops:
  7.2 58.1 %copy-start = (bf16[3,64,1024]{2,1,0:T(8,128)(2,1)S(1)}, bf16[3,64,1024]{2,1,0:T(8,128)(2,1)}, u32[]{:S(2)}) copy-start(bf16[3,64,1024]{2,1,0:T(8,128)(2,1)} %param.28) | copy-start | bytes 1179652
  7.2 13.6 %copy-start.10 = (bf16[1,4,4,1024]{3,2,1,0:T(4,128)(2,1)S(1)}, bf16[1,4,4,1024]{3,2,1,0:T(4,128)(2,1)}, u32[]{:S(2)}) copy-start(bf16[1,4,4,1024]{3,2,1,0:T(4,128)(2,1)} %param.21) | copy-start | bytes 98308
  7.2 13.8 %copy-start.21 = (f32[1024]{0:T(1024)S(1)}, f32[1024]{0:T(1024)}, u32[]{:S(2)}) copy-start(f32[1024]{0:T(1024)} %param.25) | copy-start | bytes 12292
  7.2 13.8 %copy-start.16 = (bf16[1,4,4,1024]{3,2,1,0:T(4,128)(2,1)S(1)}, bf16[1,4,4,1024]{3,2,1,0:T(4,128)(2,1)}, u32[]{:S(2)}) copy-start(bf16[1,4,4,1024]{3,2,1,0:T(4,128)(2,1)} %param.22) | copy-start | bytes 98308
  7.2 383.7 %reduce-scatter.2.cloned.1.call-start = ((), (), s32[]{:S(2)}) async-start(), calls=%async_computation.1 | async-start | bytes 557056 | tf_op jit(solution)/shard_map/reduce_scatter | solution.py:294
  9.0 0.6 copy-start.14
  10.3 55.0 %copy-start.19 = (f32[256]{0:T(256)}, f32[256]{0:T(256)S(1)}, u32[]{:S(2)}) copy-start(f32[256]{0:T(256)S(1)} %add_multiply_fusion.1) | copy-start | bytes 3076
  12.7 87.4 %copy-start.11 = (bf16[64,1024]{1,0:T(8,128)(2,1)S(1)}, bf16[64,1024]{1,0:T(8,128)(2,1)}, u32[]{:S(2)}) copy-start(bf16[64,1024]{1,0:T(8,128)(2,1)} %param.29) | copy-start | bytes 393220
  12.7 222.2 %collective-permute-start = (bf16[1,3,32,512]{3,2,1,0:T(8,128)(2,1)S(1)}, bf16[1,3,32,512]{3,2,1,0:T(8,128)(2,1)S(1)}, u32[]{:S(2)}, u32[]{:S(2)}) collective-permute-start(bf16[1,3,32,512]{3,2,1,0:T(8,128)(2,1)S(1)} %get-tuple-element.74), channel_id=1, source_target_pairs={{0,4},{4,8},{8,12},{1,5},{5,9},{9,13},{2,6},{6,10},{10,14},{3,7},{... | collective-permute-start | bytes 294920 | tf_op jit(solution)/shard_map/ppermute | solution.py:27
  19.4 215.5 %collective-permute-start.1 = (bf16[1,3,32,512]{3,2,1,0:T(8,128)(2,1)S(1)}, bf16[1,3,32,512]{3,2,1,0:T(8,128)(2,1)S(1)}, u32[]{:S(2)}, u32[]{:S(2)}) collective-permute-start(bf16[1,3,32,512]{3,2,1,0:T(8,128)(2,1)S(1)} %get-tuple-element.75), channel_id=1, source_target_pairs={{4,0},{8,4},{12,8},{5,1},{9,5},{13,9},{6,2},{10,6},{14,10},{7,3},{... | collective-permute-start | bytes 294920 | tf_op jit(solution)/shard_map/ppermute | solution.py:28
  21.0 44.3 %copy-start.17 = (f32[16]{0:T(128)}, f32[16]{0:T(128)S(1)}, u32[]{:S(2)}) copy-start(f32[16]{0:T(128)S(1)} %rsqrt.26) | copy-start | bytes 196
  21.0 79.3 %copy-start.12 = (f32[1024]{0:T(1024)}, f32[1024]{0:T(1024)S(1)}, u32[]{:S(2)}) copy-start(f32[1024]{0:T(1024)S(1)} %add_multiply_fusion) | copy-start | bytes 12292
  102.3 1.0 copy-start.6
  102.3 1.0 copy-start.9
  235.0 4.5 %collective-permute-start.2 = (bf16[1,14,3,512]{3,2,1,0:T(4,128)(2,1)S(1)}, bf16[1,14,3,512]{3,2,1,0:T(4,128)(2,1)S(1)}, u32[]{:S(2)}, u32[]{:S(2)}) collective-permute-start(bf16[1,14,3,512]{3,2,1,0:T(4,128)(2,1)S(1)} %get-tuple-element.72), channel_id=1, source_target_pairs={{0,1},{1,2},{2,3},{4,5},{5,6},{6,7},{8,9},{9,10},{10,11},{12,13},{... | collective-permute-start | bytes 129032 | tf_op jit(solution)/shard_map/ppermute | solution.py:27
  237.2 4.9 %collective-permute-start.3 = (bf16[1,14,3,512]{3,2,1,0:T(4,128)(2,1)S(1)}, bf16[1,14,3,512]{3,2,1,0:T(4,128)(2,1)S(1)}, u32[]{:S(2)}, u32[]{:S(2)}) collective-permute-start(bf16[1,14,3,512]{3,2,1,0:T(4,128)(2,1)S(1)} %get-tuple-element.73), channel_id=1, source_target_pairs={{1,0},{2,1},{3,2},{5,4},{6,5},{7,6},{9,8},{10,9},{11,10},{13,12},{... | collective-permute-start | bytes 129032 | tf_op jit(solution)/shard_map/ppermute | solution.py:28
  254.5 1.9 copy-start.1
  256.5 1.1 copy-start.2
  258.7 4.3 %copy-start.7 = (bf16[1,8,32,256]{3,2,1,0:T(8,128)(2,1)S(1)}, bf16[1,8,32,256]{3,2,1,0:T(8,128)(2,1)}, u32[]{:S(2)}) copy-start(bf16[1,8,32,256]{3,2,1,0:T(8,128)(2,1)} %param.20) | copy-start | bytes 393220
  259.8 4.3 %copy-start.4 = (bf16[4,64,4,64]{1,3,2,0:T(8,128)(2,1)S(1)}, bf16[4,64,4,64]{1,3,2,0:T(8,128)(2,1)}, u32[]{:S(2)}) copy-start(bf16[4,64,4,64]{1,3,2,0:T(8,128)(2,1)} %fusion.4) | copy-start | bytes 393220
  260.5 5.4 %collective-permute-start.4 = (f32[14,3,512]{2,1,0:T(4,128)}, f32[14,3,512]{2,1,0:T(4,128)}, u32[]{:S(2)}, u32[]{:S(2)}) collective-permute-start(f32[14,3,512]{2,1,0:T(4,128)} %get-tuple-element.63), channel_id=1, source_target_pairs={{0,1},{1,2},{2,3},{4,5},{5,6},{6,7},{8,9},{9,10},{10,11},{12,13},{... | collective-permute-start | bytes 258056 | tf_op jit(solution)/shard_map/ppermute | solution.py:36
  264.5 5.5 %collective-permute-start.5 = (f32[14,3,512]{2,1,0:T(4,128)S(1)}, f32[14,3,512]{2,1,0:T(4,128)S(1)}, u32[]{:S(2)}, u32[]{:S(2)}) collective-permute-start(f32[14,3,512]{2,1,0:T(4,128)S(1)} %get-tuple-element.62), channel_id=1, source_target_pairs={{1,0},{2,1},{3,2},{5,4},{6,5},{7,6},{9,8},{10,9},{11,10},{13,12},{... | collective-permute-start | bytes 258056 | tf_op jit(solution)/shard_map/ppermute | solution.py:36
  270.5 11.2 %copy-start.3 = (bf16[1,8,32,256]{3,2,1,0:T(8,128)(2,1)S(1)}, bf16[1,8,32,256]{3,2,1,0:T(8,128)(2,1)}, u32[]{:S(2)}) copy-start(bf16[1,8,32,256]{3,2,1,0:T(8,128)(2,1)} %param.19) | copy-start | bytes 393220
  270.5 11.2 %copy-start.15 = (f32[8,32]{1,0:T(8,128)S(1)}, f32[8,32]{1,0:T(8,128)}, u32[]{:S(2)}) copy-start(f32[8,32]{1,0:T(8,128)} %copy-done.14) | copy-start | bytes 3076
  270.5 11.2 %copy-start.20 = (f32[256]{0:T(256)S(1)}, f32[256]{0:T(256)}, u32[]{:S(2)}) copy-start(f32[256]{0:T(256)} %copy-done.19) | copy-start | bytes 3076
  270.5 4.1 %collective-permute-start.6 = (f32[3,32,512]{2,1,0:T(8,128)S(1)}, f32[3,32,512]{2,1,0:T(8,128)S(1)}, u32[]{:S(2)}, u32[]{:S(2)}) collective-permute-start(f32[3,32,512]{2,1,0:T(8,128)S(1)} %get-tuple-element.65), channel_id=1, source_target_pairs={{0,4},{4,8},{8,12},{1,5},{5,9},{9,13},{2,6},{6,10},{10,14},{3,7},{... | collective-permute-start | bytes 589832 | tf_op jit(solution)/shard_map/ppermute | solution.py:36
  272.0 9.5 %collective-permute-start.7 = (f32[3,32,512]{2,1,0:T(8,128)S(1)}, f32[3,32,512]{2,1,0:T(8,128)S(1)}, u32[]{:S(2)}, u32[]{:S(2)}) collective-permute-start(f32[3,32,512]{2,1,0:T(8,128)S(1)} %get-tuple-element.64), channel_id=1, source_target_pairs={{4,0},{8,4},{12,8},{5,1},{9,5},{13,9},{6,2},{10,6},{14,10},{7,3},{... | collective-permute-start | bytes 589832 | tf_op jit(solution)/shard_map/ppermute | solution.py:36
  281.6 1.0 copy-start.8
  282.6 1.2 copy-start.5
  282.6 108.4 %copy-start.13 = (f32[1024]{0:T(1024)S(1)}, f32[1024]{0:T(1024)}, u32[]{:S(2)}) copy-start(f32[1024]{0:T(1024)} %copy-done.12) | copy-start | bytes 12292
  282.6 109.3 %copy-start.18 = (f32[16]{0:T(128)S(1)}, f32[16]{0:T(128)}, u32[]{:S(2)}) copy-start(f32[16]{0:T(128)} %copy-done.17) | copy-start | bytes 196
Sparse Core Ops, SparseCore 0:
  102.5 103.7 reduce-scatter.1
where the time goes:
time: 401 us; the launch traced here: 400 us
  blocking collectives  316 us (79%)
  starting transfers between devices  18.3 us (5%)
  local copies, waits for them, and re-layouts  16.8 us (4%)
  between operations  15.5 us (4%)
  waiting for transfers between devices  13.7 us (3%)
  matrix products  10.7 us (3%)
  other arithmetic  8.66 us (2%)
    psum x1, blocking collectives, local(): lax.psum((coarse_qkv_local, coarse_out_local), 'batch')  131 us
    psum x1, blocking collectives, local(): lax.psum((grad_qkv_local, grad_out_local), ('batch', 'gy', 'gx'))  107 us
    all_gather x1, blocking collectives, local(): all_normed = lax.all_gather(coarse_normed, ('gy', 'gx'), axis=0, tiled=True)  44.2 us
    all_gather x1, blocking collectives, local(): all_cot = lax.all_gather(coarse_cot, ('gy', 'gx'), axis=0, tiled=True)  34 us
    ppermute x4, waiting for transfers between devices, shifted(): lax.ppermute(value, axis, [(source, source + steps) for source in range(l...  11 us
    ppermute x2, starting transfers between devices, padded_2(): before = lax.ppermute(last, axis, up)  8.95 us
  transfers between devices with their start and end apart: 9, of which 4 were waited for; matrix products, arithmetic and copies ran while one was open for 7% of the time, Pallas kernels for 0%

commit v1 on v0

v1 whole, which is shorter than its diff:
```python
import math

import jax
import jax.numpy as jnp
from jax import lax
from jax.experimental import pallas as pl
from jax.experimental.pallas import tpu as pltpu
from jax.sharding import PartitionSpec as P

D_F = 256
H_F = 4
D_C = 1024
HD = 64
RAD = 3
F32 = jnp.float32
BF16 = jnp.bfloat16
MESH = pl.DeviceIdType.MESH

eps = 1e-06
log_span = math.log(1000.0)
scale = 1.0 / math.sqrt(HD)

OWN, LEFT, RIGHT, TOP, BOTTOM, TL, TR, BL, BR = range(9)
SEGMENTS = (
    (0, 8, 32, 0, 0),
    (256, 8, 8, 0, -8),
    (320, 8, 8, 0, 32),
    (384, 3, 32, -3, 0),
    (480, 3, 32, 8, 0),
    (576, 4, 8, -4, -8),
    (608, 4, 8, -4, 32),
    (640, 4, 8, 8, -8),
    (672, 4, 8, 8, 32),
)
KEYS = 704
HALO = KEYS - 256
FROM = {LEFT: (0, -1), RIGHT: (0, 1), TOP: (-1, 0), BOTTOM: (1, 0),
        TL: (-1, -1), TR: (-1, 1), BL: (1, -1), BR: (1, 1)}
BACK = {LEFT: RIGHT, RIGHT: LEFT, TOP: BOTTOM, BOTTOM: TOP, TL: BR, BR: TL, TR: BL, BL: TR}


def nn(a, b):
    return lax.dot_general(a, b, (((1,), (0,)), ((), ())), preferred_element_type=F32)


def nt(a, b):
    return lax.dot_general(a, b, (((1,), (1,)), ((), ())), preferred_element_type=F32)


def tn(a, b):
    return lax.dot_general(a, b, (((0,), (0,)), ((), ())), preferred_element_type=F32)


def rcopy(src, dst, ssem, rsem, device):
    return pltpu.make_async_remote_copy(
        src_ref=src, dst_ref=dst, send_sem=ssem, recv_sem=rsem,
        device_id=device, device_id_type=MESH,
    )


def time_gain(gains, step_value):
    channels = gains.shape[0]
    frequency = jnp.exp(-log_span * jnp.arange(channels, dtype=F32) / channels)
    return gains * (1.0 + 0.5 * jnp.cos(step_value.astype(F32) * frequency))


def norm_backward(floats, inverse, factor, upstream):
    scaled = upstream * factor
    middle = jnp.mean(floats * scaled, axis=-1, keepdims=True)
    return (inverse * scaled - floats * inverse * inverse * inverse * middle).astype(BF16)


def kernel(
    xf, dyf, xc, dyc, ff, fc, wqkv, wout, cw, cwo,
    dxf, dxc, gfq, gfo, gcq, gco,
    ag, kv, edge, bias, nf, qm, um, kt, vt, wall, sall, att, dqt, dkv, gsend, grecv,
    rs_send, rsx, rsz_send, rsz,
    cg, cgb, cgp, c16, c16r, cfin,
    fg, fgb, fgp, f16, f16r, fone, ffin,
    s_ag, r_ag, s_h, r_h, s_g, r_g, s_rx, r_rx, s_rz, r_rz,
    s_cc, r_cc, s_c16, r_c16, s_cag, r_cag,
    s_fc, r_fc, s_f16, r_f16, s_f1, r_f1, s_fag, r_fag,
):
    b = lax.axis_index("batch")
    gy = lax.axis_index("gy")
    gx = lax.axis_index("gx")
    core = lax.rem(b, 2)
    bz = b // 2
    slot = gx * 4 + gy

    def group(p):
        return (b, lax.rem(p, 4), p // 4)

    def batch(p):
        return (p * 2 + core, gy, gx)

    partner = (b + 1 - 2 * core, gy, gx)

    barrier = pltpu.get_barrier_semaphore()

    def greet(i, carry):
        pl.semaphore_signal(barrier, inc=1, device_id=group(lax.rem(slot + i, 16)), device_id_type=MESH)
        pl.semaphore_signal(barrier, inc=1, device_id=batch(lax.rem(bz + i, 16)), device_id_type=MESH)
        return carry

    lax.fori_loop(1, 16, greet, 0)
    pl.semaphore_signal(barrier, inc=1, device_id=partner, device_id_type=MESH)

    xcf = xc[...].astype(F32)
    inv_c = lax.rsqrt(jnp.mean(xcf * xcf, axis=-1, keepdims=True) + eps)
    ag[slot, 0:16, :] = (xcf * inv_c * fc[...]).astype(BF16)
    ag[slot, 16:32, :] = dyc[...]

    xff = xf[...].astype(F32)
    inv_f = lax.rsqrt(jnp.mean(xff * xff, axis=-1, keepdims=True) + eps)
    normed = (xff * inv_f * ff[...]).astype(BF16)
    nf[...] = normed
    kvp = nn(normed, wqkv[:, 256:768])
    kv[0:256, :] = kvp.astype(BF16)
    kvp3 = kvp.reshape(8, 32, 512)
    edge[0, :, :] = kvp3[:, 0:8, :].reshape(64, 512).astype(BF16)
    edge[1, :, :] = kvp3[:, 24:32, :].reshape(64, 512).astype(BF16)

    pl.semaphore_wait(barrier, 31)

    src = {
        LEFT: edge.at[1], RIGHT: edge.at[0],
        TOP: kv.at[pl.ds(160, 96)], BOTTOM: kv.at[pl.ds(0, 96)],
        TL: edge.at[1, pl.ds(32, 32)], TR: edge.at[0, pl.ds(32, 32)],
        BL: edge.at[1, pl.ds(0, 32)], BR: edge.at[0, pl.ds(0, 32)],
    }

    def toward(step):
        return (b, lax.rem(gy + step[0] + 4, 4), lax.rem(gx + step[1] + 4, 4))

    def size(s):
        return SEGMENTS[s][1] * SEGMENTS[s][2]

    halo = []
    for s in range(1, 9):
        dy, dx = FROM[s]
        halo.append(rcopy(src[s], kv.at[pl.ds(SEGMENTS[s][0], size(s))], s_h.at[s - 1], r_h.at[s - 1],
                          toward((-dy, -dx))))

    up, down, opp = lax.rem(gy + 1, 4), lax.rem(gy + 3, 4), lax.rem(gy + 2, 4)
    right, left, far = lax.rem(gx + 1, 4), lax.rem(gx + 3, 4), lax.rem(gx + 2, 4)
    to_up, to_down = (b, up, gx), (b, down, gx)
    to_right, to_left = (b, gy, right), (b, gy, left)
    sends = []

    def ag_send(g, x, part, device):
        sl = x * 4 + g
        block = ag.at[sl] if part is None else ag.at[sl, pl.ds(16 * part, 16)]
        c = rcopy(block, block, s_ag.at[len(sends)], r_ag.at[sl, part or 0], device)
        c.start()
        sends.append(c)

    def ag_wait(g, x, part=None):
        sl = x * 4 + g
        block = ag.at[sl] if part is None else ag.at[sl, pl.ds(16 * part, 16)]
        rcopy(block, block, s_ag.at[0], r_ag.at[sl, part or 0], to_up).wait_recv()

    ag_send(gy, gx, None, to_up)
    ag_send(gy, gx, None, to_down)
    for s in (TOP, BOTTOM, LEFT, RIGHT, TL, TR, BL, BR):
        halo[s - 1].start()
    ag_send(gy, gx, None, to_right)
    ag_send(gy, gx, None, to_left)

    q = nn(normed, wqkv[:, 0:256])
    upst = nt(dyf[...], wout[...])
    lane = lax.broadcasted_iota(jnp.int32, (256, 256), 1) // HD
    for h in range(H_F):
        qm[h * 256:(h + 1) * 256, :] = jnp.where(lane == h, q, 0.0).astype(BF16)
        um[h * 256:(h + 1) * 256, :] = jnp.where(lane == h, upst, 0.0).astype(BF16)
    ok_side = {OWN: None, LEFT: gx > 0, RIGHT: gx < 3, TOP: gy > 0, BOTTOM: gy < 3,
               TL: (gx > 0) & (gy > 0), TR: (gx < 3) & (gy > 0),
               BL: (gx > 0) & (gy < 3), BR: (gx < 3) & (gy < 3)}
    for s, (first, rows, cols, row0, col0) in enumerate(SEGMENTS):
        n = rows * cols
        key = lax.broadcasted_iota(jnp.int32, (n, 256), 0)
        query = lax.broadcasted_iota(jnp.int32, (n, 256), 1)
        dr = key // cols + row0 - query // 32
        dc = lax.rem(key, cols) + col0 - lax.rem(query, 32)
        ok = (dr >= -RAD) & (dr <= RAD) & (dc >= -RAD) & (dc <= RAD)
        floor = jnp.where(ok, 0.0, -1e30).astype(F32)
        if ok_side[s] is not None:
            floor = jnp.minimum(floor, jnp.where(ok_side[s], 0.0, -1e30).astype(F32))
        bias[first:first + n, :] = floor

    def relay_near():
        ag_wait(down, gx)
        ag_send(down, gx, 0, to_up)
        ag_send(down, gx, None, to_right)
        ag_send(down, gx, None, to_left)
        ag_wait(up, gx)
        ag_send(up, gx, 1, to_down)
        ag_send(up, gx, None, to_right)
        ag_send(up, gx, None, to_left)
        ag_wait(gy, left)
        ag_send(gy, left, 0, to_right)
        ag_wait(gy, right)
        ag_send(gy, right, 1, to_left)

    def relay_opposite():
        ag_wait(opp, gx, 0)
        ag_wait(opp, gx, 1)
        ag_send(opp, gx, None, to_right)
        ag_send(opp, gx, None, to_left)

    def relay_side():
        for g in (down, up):
            ag_wait(g, left)
            ag_send(g, left, 0, to_right)
            ag_wait(g, right)
            ag_send(g, right, 1, to_left)

    def relay_last():
        ag_wait(opp, left)
        ag_send(opp, left, 0, to_right)
        ag_wait(opp, right)
        ag_send(opp, right, 1, to_left)

    relay_near()
    for c in halo:
        c.wait_recv()

    kt[...] = kv[:, 0:256].T
    vt[...] = kv[:, 256:512].T

    relays = (relay_opposite, relay_side, relay_last, lambda: None)
    for h in range(H_F):
        rows = slice(h * 64, (h + 1) * 64)
        heads = slice(h * 256, (h + 1) * 256)
        s = nt(kv[:, 0:256], qm[heads, :]) * scale + bias[...]
        top = jnp.max(s, axis=0, keepdims=True)
        e = jnp.exp(s - top)
        p = e * (1.0 / jnp.sum(e, axis=0, keepdims=True))
        w = p.astype(BF16)
        wall[:, heads] = w
        dp = nt(kv[:, 256:512], um[heads, :])
        delta = jnp.sum(p * dp, axis=0, keepdims=True)
        slope = (p * (dp - delta)).astype(BF16)
        sall[:, heads] = slope
        att[rows, :] = nn(vt[rows, :], w).astype(BF16)
        dqt[rows, :] = nn(kt[rows, :], slope) * scale
        relays[h]()

    gsend[:, 0:256] = nn(sall[256:KEYS, :], qm[...]).astype(BF16)
    gsend[:, 256:512] = nn(wall[256:KEYS, :], um[...]).astype(BF16)
    ghalo = []
    for s in range(1, 9):
        dy, dx = FROM[s]
        o = BACK[s]
        c = rcopy(gsend.at[pl.ds(SEGMENTS[s][0] - 256, size(s))],
                  grecv.at[pl.ds(SEGMENTS[o][0] - 256, size(o))],
                  s_g.at[s - 1], r_g.at[s - 1], toward((dy, dx)))
        c.start()
        ghalo.append(c)
    dkv[:, :, 0:256] = nn(sall[0:256, :], qm[...]).reshape(8, 32, 256)
    dkv[:, :, 256:512] = nn(wall[0:256, :], um[...]).reshape(8, 32, 256)
    fgo = nn(att[...], dyf[...])

    for g in range(4):
        ag_wait(g, far, 0)
        ag_wait(g, far, 1)
    nall = ag[:, 0:16, :].reshape(256, D_C)
    call = ag[:, 16:32, :].reshape(256, D_C)
    proj = nt(cw[...], nall).astype(BF16)
    cqt, ckt, cvt = proj[0:64], proj[64:128], proj[128:192]
    cut = nt(cwo[...], call).astype(BF16)
    cs = tn(ckt, cqt) * scale
    ce = jnp.exp(cs - jnp.max(cs, axis=0, keepdims=True))
    cp = ce * (1.0 / jnp.sum(ce, axis=0, keepdims=True))
    cwt = cp.astype(BF16)
    cot = nn(cvt, cwt).astype(BF16)
    cdp = tn(cvt, cut)
    cdelta = jnp.sum(cp * cdp, axis=0, keepdims=True)
    cslope = (cp * (cdp - cdelta)).astype(BF16)
    cdt = jnp.concatenate(
        [nn(ckt, cslope) * scale, nt(cqt, cslope) * scale, nt(cut, cwt)], axis=0
    ).astype(BF16)
    rs_send[...] = tn(cdt, cw[...]).astype(BF16).reshape(4, 4, 16, D_C)
    rx = []
    for i in (1, 3, 2):
        x = lax.rem(gx + i, 4)
        c = rcopy(rs_send.at[x], rsx.at[i], s_rx.at[i], r_rx.at[i], (b, gy, x))
        c.start()
        rx.append(c)
    cgq = nn(cdt, nall)
    cgo = nn(cot, call)
    for half in range(2):
        lanes = slice(half * 512, (half + 1) * 512)
        cg[half, 0:192, :] = cgq[:, lanes]
        cg[half, 192:256, :] = cgo[:, lanes]
        cgb[half, 0:192, :] = cgq[:, lanes].astype(BF16)
        cgb[half, 192:256, :] = cgo[:, lanes].astype(BF16)
    cc = rcopy(cgb.at[1 - core], cgp, s_cc.at[0], r_cc.at[0], partner)
    cc.start()

    for c in ghalo:
        c.wait_recv()

    def owed(s):
        first, rows, cols = SEGMENTS[s][:3]
        return grecv[first - 256:first - 256 + rows * cols, :].astype(F32).reshape(rows, cols, 512)

    dkv[:, 0:8, :] += owed(LEFT)
    dkv[:, 24:32, :] += owed(RIGHT)
    dkv[0:3, :, :] += owed(TOP)
    dkv[5:8, :, :] += owed(BOTTOM)
    dkv[0:4, 0:8, :] += owed(TL)
    dkv[0:4, 24:32, :] += owed(TR)
    dkv[4:8, 0:8, :] += owed(BL)
    dkv[4:8, 24:32, :] += owed(BR)
    dq = dqt[...].T.astype(BF16)
    dk = (dkv[:, :, 0:256].reshape(256, 256) * scale).astype(BF16)
    dv = dkv[:, :, 256:512].reshape(256, 256).astype(BF16)
    nft = nf[...].T
    fgq = nn(nft, dq)
    fgk = nn(nft, dk)
    fgv = nn(nft, dv)
    for half, (a, z) in enumerate(((fgq, fgk), (fgv, fgo))):
        fg[half, :, 0:256] = a
        fg[half, :, 256:512] = z
        fgb[half, :, 0:256] = a.astype(BF16)
        fgb[half, :, 256:512] = z.astype(BF16)
    fcc = rcopy(fgb.at[1 - core], fgp, s_fc.at[0], r_fc.at[0], partner)
    fcc.start()
    dn = nt(dq, wqkv[:, 0:256]) + nt(dk, wqkv[:, 256:512]) + nt(dv, wqkv[:, 512:768])
    xff = xf[...].astype(F32)
    inv_f = lax.rsqrt(jnp.mean(xff * xff, axis=-1, keepdims=True) + eps)
    dxf[...] = norm_backward(xff, inv_f, ff[...], dn)

    def spread(source, dest, ssem, rsem, me, device, each):
        def body(i, carry):
            p = lax.rem(me + i, 16)
            rcopy(source.at[p] if each else source, dest.at[me], ssem.at[i], rsem.at[me], device(p)).start()
            return carry
        lax.fori_loop(1, 16, body, 0)

    def collect(source, dest, ssem, rsem, me, device, each):
        def body(i, carry):
            p = lax.rem(me + i, 16)
            c = rcopy(source.at[p] if each else source, dest.at[p], ssem.at[i], rsem.at[p], device(p))
            c.wait_send()
            c.wait_recv()
            return carry
        lax.fori_loop(1, 16, body, 0)

    def total(dest):
        acc = dest[0].astype(F32)
        for i in range(1, 16):
            acc = acc + dest[i].astype(F32)
        return acc

    cc.wait_recv()
    c16[...] = (cg[core] + cgp[...].astype(F32)).astype(BF16).reshape(16, 16, 512)
    c16r[bz] = c16[bz]
    spread(c16, c16r, s_c16, r_c16, bz, batch, True)

    fcc.wait_recv()
    f16[...] = (fg[core] + fgp[...].astype(F32)).astype(BF16).reshape(16, 16, 512)
    f16r[slot] = f16[slot]
    spread(f16, f16r, s_f16, r_f16, slot, group, True)

    acc = rs_send[gx].astype(F32)
    for i, c in zip((1, 3, 2), rx):
        c.wait_recv()
        acc = acc + rsx[i].astype(F32)
    rsz_send[...] = acc.astype(BF16)
    rz = []
    for i in (1, 3, 2):
        g = lax.rem(gy + i, 4)
        c = rcopy(rsz_send.at[g], rsz.at[i], s_rz.at[i], r_rz.at[i], (b, g, gx))
        c.start()
        rz.append(c)

    collect(c16, c16r, s_c16, r_c16, bz, batch, True)
    cmine = cfin.at[core, bz]
    cmine[...] = total(c16r).astype(BF16)
    spread(cmine, cfin.at[core], s_cag, r_cag, bz, batch, False)

    collect(f16, f16r, s_f16, r_f16, slot, group, True)
    fone[bz] = total(f16r).astype(BF16)
    spread(fone.at[bz], fone, s_f1, r_f1, bz, batch, False)

    dnc = rsz_send[gy].astype(F32)
    for i, c in zip((1, 3, 2), rz):
        c.wait_recv()
        dnc = dnc + rsz[i].astype(F32)
    xcf = xc[...].astype(F32)
    inv_c = lax.rsqrt(jnp.mean(xcf * xcf, axis=-1, keepdims=True) + eps)
    dxc[...] = norm_backward(xcf, inv_c, fc[...], dnc)

    collect(cmine, cfin.at[core], s_cag, r_cag, bz, batch, False)
    cc2 = rcopy(cfin.at[core], cfin.at[core], s_cc.at[1], r_cc.at[1], partner)
    cc2.start()

    collect(fone.at[bz], fone, s_f1, r_f1, bz, batch, False)
    fmine = ffin.at[core, slot]
    fmine[...] = total(fone).astype(BF16)
    spread(fmine, ffin.at[core], s_fag, r_fag, slot, group, False)

    rcopy(cfin.at[1 - core], cfin.at[1 - core], s_cc.at[1], r_cc.at[1], partner).wait_recv()
    for half in range(2):
        lanes = slice(half * 512, (half + 1) * 512)
        done = cfin[half].reshape(256, 512)
        gcq[:, lanes] = done[0:192]
        gco[:, lanes] = done[192:256]

    collect(fmine, ffin.at[core], s_fag, r_fag, slot, group, False)
    fc2 = rcopy(ffin.at[core], ffin.at[core], s_fc.at[1], r_fc.at[1], partner)
    fc2.start()
    rcopy(ffin.at[1 - core], ffin.at[1 - core], s_fc.at[1], r_fc.at[1], partner).wait_recv()
    gfq[:, 0:512] = ffin[0].reshape(256, 512)
    done = ffin[1].reshape(256, 512)
    gfq[:, 512:768] = done[:, 0:256]
    gfo[...] = done[:, 256:512]

    for c in sends + halo + ghalo + rx + rz + [cc, fcc, cc2, fc2]:
        c.wait_send()


def local(x_fine, dy_fine, x_coarse, dy_coarse, timestep, fine_gain, coarse_gain,
          fine_qkv, fine_out, coarse_qkv, coarse_out):
    t = timestep[0]
    vm = pl.BlockSpec(memory_space=pltpu.VMEM)
    dma = pltpu.SemaphoreType.DMA
    V = pltpu.VMEM
    outs = (
        jax.ShapeDtypeStruct((256, 256), BF16),
        jax.ShapeDtypeStruct((16, D_C), BF16),
        jax.ShapeDtypeStruct((256, 768), BF16),
        jax.ShapeDtypeStruct((256, 256), BF16),
        jax.ShapeDtypeStruct((192, D_C), BF16),
        jax.ShapeDtypeStruct((64, D_C), BF16),
    )
    scratch = [
        V((16, 32, D_C), BF16), V((KEYS, 512), BF16), V((2, 64, 512), BF16), V((KEYS, 256), F32),
        V((256, 256), BF16), V((1024, 256), BF16), V((1024, 256), BF16),
        V((256, KEYS), BF16), V((256, KEYS), BF16), V((KEYS, 1024), BF16), V((KEYS, 1024), BF16),
        V((256, 256), BF16), V((256, 256), F32), V((8, 32, 512), F32),
        V((HALO, 512), BF16), V((HALO, 512), BF16),
        V((4, 4, 16, D_C), BF16), V((4, 4, 16, D_C), BF16), V((4, 16, D_C), BF16), V((4, 16, D_C), BF16),
        V((2, 256, 512), F32), V((2, 256, 512), BF16), V((256, 512), BF16),
        V((16, 16, 512), BF16), V((16, 16, 512), BF16), V((2, 16, 16, 512), BF16),
        V((2, 256, 512), F32), V((2, 256, 512), BF16), V((256, 512), BF16),
        V((16, 16, 512), BF16), V((16, 16, 512), BF16), V((16, 16, 512), BF16), V((2, 16, 16, 512), BF16),
        dma((24,)), dma((16, 2)), dma((8,)), dma((8,)), dma((8,)), dma((8,)),
        dma((4,)), dma((4,)), dma((4,)), dma((4,)),
        dma((2,)), dma((2,)), dma((16,)), dma((16,)), dma((16,)), dma((16,)),
        dma((2,)), dma((2,)), dma((16,)), dma((16,)), dma((16,)), dma((16,)), dma((16,)), dma((16,)),
    ]
    dxf, dxc, gfq, gfo, gcq, gco = pl.pallas_call(
        kernel,
        out_shape=outs,
        in_specs=[vm] * 10,
        out_specs=[vm] * 6,
        scratch_shapes=scratch,
        compiler_params=pltpu.CompilerParams(
            collective_id=0, has_side_effects=True, vmem_limit_bytes=50 * 1024 * 1024
        ),
    )(
        x_fine.reshape(256, D_F), dy_fine.reshape(256, D_F),
        x_coarse.reshape(16, D_C), dy_coarse.reshape(16, D_C),
        time_gain(fine_gain, t)[None], time_gain(coarse_gain, t)[None],
        fine_qkv, fine_out, coarse_qkv.reshape(192, D_C), coarse_out,
    )
    return (
        dxf.reshape(x_fine.shape),
        dxc.reshape(x_coarse.shape),
        gfq,
        gfo,
        gcq.reshape(coarse_qkv.shape),
        gco,
    )


def solution(mesh):
    tile = P("batch", "gy", "gx", None)
    heads = P(None, ("gy", "gx"), None)
    rows = P(("gy", "gx"), None)
    return jax.shard_map(
        local,
        mesh=mesh,
        in_specs=(tile, tile, tile, tile, P("batch"), P(), P(), P(), P(), heads, rows),
        out_specs=(tile, tile, P(), P(), heads, rows),
        check_vma=False,
    )
```

time: 401 us -> 97.5 us (0.24)
  blocking collectives: 316 us -> 0 us
  Pallas kernels: 0 us -> 83.9 us
  starting transfers between devices: 18.3 us -> 0 us
  between operations: 15.5 us -> 1.36 us
  waiting for transfers between devices: 13.7 us -> 0 us
  matrix products: 10.7 us -> 0 us
  other arithmetic: 8.66 us -> 1.48 us
  local copies, waits for them, and re-layouts: 16.8 us -> 10.3 us
    psum x2 -> x0, blocking collectives: 238 us -> none  [the longest x1 131 us: local(): lax.psum((coarse_qkv_local, coarse_out_local), 'batch')]
    pallas_call x0 -> x1, Pallas kernels: none -> 83.9 us  [local(): pl.pallas_call(kernel, out_shape=outs, in_specs=[vm] * 10, out_specs=[vm]...]
    all_gather x2 -> x0, blocking collectives: 78.2 us -> none  [the longest x1 44.2 us: local(): all_normed = lax.all_gather(coarse_normed, ('gy', 'gx'), axis=0, tiled=True)]
    ppermute x8 -> x0, starting transfers between devices: 18.3 us -> none  [the longest x2 8.95 us: padded_2(): before = lax.ppermute(last, axis, up)]
    ppermute x8 -> x0, waiting for transfers between devices: 13.7 us -> none  [the longest x4 11 us: shifted(): lax.ppermute(value, axis, [(source, source + steps) for source in range(l...]
    dot_general x21 -> x0, matrix products: 10.7 us -> none  [the longest x16 7.55 us: contract(): jnp.einsum(pattern, first_op, second_op, preferred_element_type=jnp.float32)]
    unnamed x45 -> x17, local copies, waits for them, and re-layouts: 2.25 us -> 8.16 us
    transpose x6 -> x0, local copies, waits for them, and re-layouts: 4.17 us -> none  [the longest x2 3.11 us: contract(): jnp.einsum(pattern, first_op, second_op, preferred_element_type=jnp.float32)]
  transfers between devices with their start and end apart: 9 -> 0, of which waited for: 4 -> 0; matrix products, arithmetic and copies ran while one was open for 7% -> 0% of each run, Pallas kernels for 0% -> 0%
where the time goes in v1:
time: 97.5 us; the launch traced here: 97 us
  Pallas kernels  83.9 us (86%)
  local copies, waits for them, and re-layouts  10.3 us (11%)
  other arithmetic  1.48 us (2%)
  between operations  1.36 us (1%)
    pallas_call x1, Pallas kernels, local(): pl.pallas_call(kernel, out_shape=outs, in_specs=[vm] * 10, out_specs=[vm]...  83.9 us
    unnamed x17, local copies, waits for them, and re-layouts  8.16 us

profile of v1, /device:TPU:1, one launch (start us, length us, event | category | flops | bytes accessed | tf_op | source)
XLA Modules:
  0.0 97.0 jit_solution(10969343335363400906)
XLA Ops:
  0.6 0.0 copy-start.2
  1.3 0.7 add_multiply_fusion.1
  2.1 0.7 add_multiply_fusion
  2.8 0.8 reshape.39.xc
  3.6 0.8 reshape.40.dyc
  4.4 0.0 copy-done.2
  4.4 0.0 copy-start
  4.4 1.0 %copy-done = bf16[256,768]{1,0:T(8,128)(2,1)S(1)} copy-done((bf16[256,768]{1,0:T(8,128)(2,1)S(1)}, bf16[256,768]{1,0:T(8,128)(2,1)}, u32[]{:S(2)}) %copy-start) | copy-done | bytes 393240
  5.4 0.0 copy-start.1
  5.4 1.0 %copy-done.1 = bf16[3,64,1024]{2,1,0:T(8,128)(2,1)S(1)} copy-done((bf16[3,64,1024]{2,1,0:T(8,128)(2,1)S(1)}, bf16[3,64,1024]{2,1,0:T(8,128)(2,1)}, u32[]{:S(2)}) %copy-start.1) | copy-done | bytes 393240
  6.4 0.0 copy-start.3
  6.4 0.9 copy-done.3
  7.3 0.0 copy-start.4
  7.3 0.9 copy-done.4
  8.2 0.0 copy-start.5
  8.2 0.9 copy-done.5
  9.1 83.9 %shard_map.154 = (bf16[256,256]{1,0:T(8,128)(2,1)S(1)}, bf16[16,1024]{1,0:T(8,128)(2,1)S(1)}, bf16[256,768]{1,0:T(8,128)(2,1)S(1)}, bf16[256,256]{1,0:T(8,128)(2...) custom-call(bf16[256,256]{1,0:T(8,128)(2,1)S(1)} %bitcast.10, bf16[256,256]{1,0:T(8,128)(2,1)S(1)} %bitcast.11, ...), custom_call_target="tpu_custom_call" | custom-call | tf_op jit(solution)/shard_map/pallas_call | solution.py:455
  92.9 0.6 reshape.43
  93.6 0.7 copy.23
  94.2 0.7 copy.24
  95.0 0.7 copy.25
  95.6 0.7 copy.26
  96.4 0.7 copy.27
Async XLA Ops:
  0.6 3.7 %copy-start.2 = (bf16[1,8,32,256]{3,2,1,0:T(8,128)(2,1)S(1)}, bf16[1,8,32,256]{3,2,1,0:T(8,128)(2,1)}, u32[]{:S(2)}) copy-start(bf16[1,8,32,256]{3,2,1,0:T(8,128)(2,1)} %param.11) | copy-start | bytes 393220
  4.4 1.0 %copy-start = (bf16[256,768]{1,0:T(8,128)(2,1)S(1)}, bf16[256,768]{1,0:T(8,128)(2,1)}, u32[]{:S(2)}) copy-start(bf16[256,768]{1,0:T(8,128)(2,1)} %wqkv.1) | copy-start | bytes 1179652
  5.4 1.0 %copy-start.1 = (bf16[3,64,1024]{2,1,0:T(8,128)(2,1)S(1)}, bf16[3,64,1024]{2,1,0:T(8,128)(2,1)}, u32[]{:S(2)}) copy-start(bf16[3,64,1024]{2,1,0:T(8,128)(2,1)} %param.20) | copy-start | bytes 1179652
  6.4 0.9 copy-start.3
  7.3 0.9 copy-start.4
  8.2 0.9 copy-start.5

commit v2 on v1

v2 whole, which is shorter than its diff:
```python
import math

import jax
import jax.numpy as jnp
from jax import lax
from jax.experimental import pallas as pl
from jax.experimental.pallas import tpu as pltpu
from jax.sharding import PartitionSpec as P

D_F = 256
H_F = 4
D_C = 1024
HD = 64
RAD = 3
F32 = jnp.float32
BF16 = jnp.bfloat16
MESH = pl.DeviceIdType.MESH

eps = 1e-06
log_span = math.log(1000.0)
scale = 1.0 / math.sqrt(HD)

OWN, LEFT, RIGHT, TOP, BOTTOM, TL, TR, BL, BR = range(9)
SEGMENTS = (
    (0, 8, 32, 0, 0),
    (256, 8, 8, 0, -8),
    (320, 8, 8, 0, 32),
    (384, 3, 32, -3, 0),
    (480, 3, 32, 8, 0),
    (576, 4, 8, -4, -8),
    (608, 4, 8, -4, 32),
    (640, 4, 8, 8, -8),
    (672, 4, 8, 8, 32),
)
KEYS = 704
HALO = KEYS - 256
FROM = {LEFT: (0, -1), RIGHT: (0, 1), TOP: (-1, 0), BOTTOM: (1, 0),
        TL: (-1, -1), TR: (-1, 1), BL: (1, -1), BR: (1, 1)}
BACK = {LEFT: RIGHT, RIGHT: LEFT, TOP: BOTTOM, BOTTOM: TOP, TL: BR, BR: TL, TR: BL, BL: TR}


def nn(a, b):
    return lax.dot_general(a, b, (((1,), (0,)), ((), ())), preferred_element_type=F32)


def nt(a, b):
    return lax.dot_general(a, b, (((1,), (1,)), ((), ())), preferred_element_type=F32)


def tn(a, b):
    return lax.dot_general(a, b, (((0,), (0,)), ((), ())), preferred_element_type=F32)


def mark(name):
    pass


def rcopy(src, dst, ssem, rsem, device):
    return pltpu.make_async_remote_copy(
        src_ref=src, dst_ref=dst, send_sem=ssem, recv_sem=rsem,
        device_id=device, device_id_type=MESH,
    )


def time_gain(gains, step_value):
    channels = gains.shape[1]
    place = lax.broadcasted_iota(jnp.int32, (8, channels), 1).astype(F32)
    frequency = jnp.exp(-log_span * place / channels)
    factor = jnp.cos(step_value * frequency)
    return gains * (1.0 + 0.5 * factor[0:1])


def norm_backward(floats, inverse, factor, upstream):
    scaled = upstream * factor
    middle = jnp.mean(floats * scaled, axis=-1, keepdims=True)
    return (inverse * scaled - floats * inverse * inverse * inverse * middle).astype(BF16)


def kernel(
    t_ref, xf_h, dyf_h, xc_h, dyc_h, gf_h, gc_h, wqkv_h, wout_h, cw_h, cwo_h,
    dxf, dxc, gfq, gfo, gcq, gco,
    xf, dyf, xc4, dyc4, gf, gc, wqkv, wout, cw, cwo, xc, ff, fc,
    ag, nrm, kv, edge, bias, qm, um, kt, vt, nt_all, wall, sall, att, dqt, dn, gsend, grecv,
    rs_send, rsx, rsz_send, rsz,
    cg, cgb, cgp, c16, c16r, cfin,
    fg, fgb, fgp, f16, f16r, fone, ffin,
    s_in, s_ag, r_ag, s_h, r_h, s_g, r_g, s_rx, r_rx, s_rz, r_rz,
    s_cc, r_cc, s_c16, r_c16, s_cag, r_cag, s_cf, r_cf,
    s_fc, r_fc, s_f16, r_f16, s_f1, r_f1, s_fag, r_fag, s_ff, r_ff,
):
    b = lax.axis_index("batch")
    gy = lax.axis_index("gy")
    gx = lax.axis_index("gx")
    core = lax.rem(b, 2)
    bz = b // 2
    slot = gx * 4 + gy

    def group(p):
        return (b, lax.rem(p, 4), p // 4)

    def batch(p):
        return (p * 2 + core, gy, gx)

    partner = (b + 1 - 2 * core, gy, gx)

    mark("greet")
    loads = [
        pltpu.make_async_copy(h, v, s_in.at[i])
        for i, (h, v) in enumerate((
            (gf_h, gf), (gc_h, gc), (xf_h, xf), (xc_h, xc4), (dyc_h, dyc4), (wqkv_h, wqkv), (wout_h, wout),
            (dyf_h, dyf), (cw_h, cw), (cwo_h, cwo),
        ))
    ]
    for c in loads:
        c.start()
    barrier = pltpu.get_barrier_semaphore()

    def greet(i, carry):
        pl.semaphore_signal(barrier, inc=1, device_id=group(lax.rem(slot + i, 16)), device_id_type=MESH)
        pl.semaphore_signal(barrier, inc=1, device_id=batch(lax.rem(bz + i, 16)), device_id_type=MESH)
        return carry

    lax.fori_loop(1, 16, greet, 0)
    pl.semaphore_signal(barrier, inc=1, device_id=partner, device_id_type=MESH)

    mark("norms")
    step_value = t_ref[0].astype(F32)
    for c in loads[0:3]:
        c.wait()
    ff[...] = time_gain(gf[...], step_value)
    fc[...] = time_gain(gc[...], step_value)

    xff = xf[...].astype(F32)
    inv_f = lax.rsqrt(jnp.mean(xff * xff, axis=-1, keepdims=True) + eps)
    normf = xff * inv_f * ff[...]
    normed = normf.astype(BF16)
    nrm[0:256, :] = normed
    norm3 = normf.reshape(8, 32, 256)
    edge[0, :, :] = norm3[:, 0:8, :].reshape(64, 256).astype(BF16)
    edge[1, :, :] = norm3[:, 24:32, :].reshape(64, 256).astype(BF16)

    for c in loads[3:5]:
        c.wait()
    for r in range(4):
        xc[4 * r:4 * r + 4, :] = xc4[r].astype(F32)
    xcf = xc[...]
    inv_c = lax.rsqrt(jnp.mean(xcf * xcf, axis=-1, keepdims=True) + eps)
    ag[slot, 0:16, :] = (xcf * inv_c * fc[...]).astype(BF16)
    ag[slot, 16:32, :] = jnp.concatenate([dyc4[r].astype(F32) for r in range(4)], axis=0).astype(BF16)

    mark("barwait")
    pl.semaphore_wait(barrier, 31)

    mark("send0")
    src = {
        LEFT: edge.at[1], RIGHT: edge.at[0],
        TOP: nrm.at[pl.ds(160, 96)], BOTTOM: nrm.at[pl.ds(0, 96)],
        TL: edge.at[1, pl.ds(32, 32)], TR: edge.at[0, pl.ds(32, 32)],
        BL: edge.at[1, pl.ds(0, 32)], BR: edge.at[0, pl.ds(0, 32)],
    }

    def toward(step):
        return (b, lax.rem(gy + step[0] + 4, 4), lax.rem(gx + step[1] + 4, 4))

    def size(s):
        return SEGMENTS[s][1] * SEGMENTS[s][2]

    halo = []
    for s in range(1, 9):
        dy, dx = FROM[s]
        halo.append(rcopy(src[s], nrm.at[pl.ds(SEGMENTS[s][0], size(s))], s_h.at[s - 1], r_h.at[s - 1],
                          toward((-dy, -dx))))

    up, down, opp = lax.rem(gy + 1, 4), lax.rem(gy + 3, 4), lax.rem(gy + 2, 4)
    right, left, far = lax.rem(gx + 1, 4), lax.rem(gx + 3, 4), lax.rem(gx + 2, 4)
    to_up, to_down = (b, up, gx), (b, down, gx)
    to_right, to_left = (b, gy, right), (b, gy, left)
    sends = []

    def ag_send(g, x, part, device):
        sl = x * 4 + g
        block = ag.at[sl] if part is None else ag.at[sl, pl.ds(16 * part, 16)]
        c = rcopy(block, block, s_ag.at[len(sends)], r_ag.at[sl, part or 0], device)
        c.start()
        sends.append(c)

    def ag_wait(g, x, part=None):
        sl = x * 4 + g
        block = ag.at[sl] if part is None else ag.at[sl, pl.ds(16 * part, 16)]
        rcopy(block, block, s_ag.at[0], r_ag.at[sl, part or 0], to_up).wait_recv()

    for s in (TL, TR, BL, BR, TOP, BOTTOM, LEFT, RIGHT):
        halo[s - 1].start()
    ag_send(gy, gx, None, to_up)
    ag_send(gy, gx, None, to_down)
    ag_send(gy, gx, None, to_right)
    ag_send(gy, gx, None, to_left)

    mark("qmask")
    for c in loads[5:8]:
        c.wait()
    kv[0:256, :] = nn(normed, wqkv[:, 256:768]).astype(BF16)
    q = nn(normed, wqkv[:, 0:256])
    upst = nt(dyf[...], wout[...])
    lane = lax.broadcasted_iota(jnp.int32, (256, 256), 1) // HD
    for h in range(H_F):
        qm[h * 256:(h + 1) * 256, :] = jnp.where(lane == h, q, 0.0).astype(BF16)
        um[h * 256:(h + 1) * 256, :] = jnp.where(lane == h, upst, 0.0).astype(BF16)
    ok_side = {OWN: None, LEFT: gx > 0, RIGHT: gx < 3, TOP: gy > 0, BOTTOM: gy < 3,
               TL: (gx > 0) & (gy > 0), TR: (gx < 3) & (gy > 0),
               BL: (gx > 0) & (gy < 3), BR: (gx < 3) & (gy < 3)}
    for s, (first, rows, cols, row0, col0) in enumerate(SEGMENTS):
        n = rows * cols
        key = lax.broadcasted_iota(jnp.int32, (n, 256), 0)
        query = lax.broadcasted_iota(jnp.int32, (n, 256), 1)
        dr = key // cols + row0 - query // 32
        dc = lax.rem(key, cols) + col0 - lax.rem(query, 32)
        ok = (dr >= -RAD) & (dr <= RAD) & (dc >= -RAD) & (dc <= RAD)
        floor = jnp.where(ok, 0.0, -1e30).astype(F32)
        if ok_side[s] is not None:
            floor = jnp.minimum(floor, jnp.where(ok_side[s], 0.0, -1e30).astype(F32))
        bias[first:first + n, :] = floor

    def relay_near():
        ag_wait(gy, left)
        ag_send(gy, left, 0, to_right)
        ag_wait(gy, right)
        ag_send(gy, right, 1, to_left)
        ag_wait(down, gx)
        ag_send(down, gx, 0, to_up)
        ag_send(down, gx, None, to_right)
        ag_send(down, gx, None, to_left)
        ag_wait(up, gx)
        ag_send(up, gx, 1, to_down)
        ag_send(up, gx, None, to_right)
        ag_send(up, gx, None, to_left)

    def relay_opposite():
        ag_wait(opp, gx, 0)
        ag_wait(opp, gx, 1)
        ag_send(opp, gx, None, to_right)
        ag_send(opp, gx, None, to_left)

    def relay_side():
        for g in (down, up):
            ag_wait(g, left)
            ag_send(g, left, 0, to_right)
            ag_wait(g, right)
            ag_send(g, right, 1, to_left)

    def relay_last():
        ag_wait(opp, left)
        ag_send(opp, left, 0, to_right)
        ag_wait(opp, right)
        ag_send(opp, right, 1, to_left)

    mark("halowait")
    for c in halo:
        c.wait_recv()

    mark("transp")
    kv[256:KEYS, :] = nn(nrm[256:KEYS, :], wqkv[:, 256:768]).astype(BF16)
    kt[...] = kv[:, 0:256].T
    vt[...] = kv[:, 256:512].T

    def head(h):
        rows = slice(h * 64, (h + 1) * 64)
        heads = slice(h * 256, (h + 1) * 256)
        s = nt(kv[:, 0:256], qm[heads, :]) * scale + bias[...]
        top = jnp.max(s, axis=0, keepdims=True)
        e = jnp.exp(s - top)
        p = e * (1.0 / jnp.sum(e, axis=0, keepdims=True))
        w = p.astype(BF16)
        wall[:, heads] = w
        dp = nt(kv[:, 256:512], um[heads, :])
        delta = jnp.sum(p * dp, axis=0, keepdims=True)
        slope = (p * (dp - delta)).astype(BF16)
        sall[:, heads] = slope
        att[rows, :] = nn(vt[rows, :], w).astype(BF16)
        dqt[rows, :] = nn(kt[rows, :], slope) * scale

    mark("head01")
    head(0)
    head(1)
    mark("relaynear")
    relay_near()
    mark("head23")
    head(2)
    head(3)

    mark("finegrad")
    nt_all[...] = nrm[...].T
    dq = dqt[...].T.astype(BF16)
    dk = (nn(sall[...], qm[...]) * scale).astype(BF16)
    dv = nn(wall[...], um[...]).astype(BF16)
    parts = (
        (nn(nt_all[:, 0:256], dq), nn(nt_all[...], dk)),
        (nn(nt_all[...], dv), nn(att[...], dyf[...])),
    )
    for half in range(2):
        for i in range(2):
            fg[half, :, 256 * i:256 * (i + 1)] = parts[half][i]
            fgb[half, :, 256 * i:256 * (i + 1)] = parts[half][i].astype(BF16)
    fcc = rcopy(fgb.at[1 - core], fgp, s_fc.at[0], r_fc.at[0], partner)
    fcc.start()

    mark("gsend")
    gsend[...] = (nt(dk[256:KEYS], wqkv[:, 256:512]) + nt(dv[256:KEYS], wqkv[:, 512:768])).astype(BF16)
    ghalo = []
    for s in range(1, 9):
        dy, dx = FROM[s]
        o = BACK[s]
        c = rcopy(gsend.at[pl.ds(SEGMENTS[s][0] - 256, size(s))],
                  grecv.at[pl.ds(SEGMENTS[o][0] - 256, size(o))],
                  s_g.at[s - 1], r_g.at[s - 1], toward((dy, dx)))
        c.start()
        ghalo.append(c)
    dn[...] = (
        nt(dq, wqkv[:, 0:256]) + nt(dk[0:256], wqkv[:, 256:512]) + nt(dv[0:256], wqkv[:, 512:768])
    ).reshape(8, 32, 256)

    def spread(source, dest, ssem, rsem, me, device, each):
        def body(i, carry):
            p = lax.rem(me + i, 16)
            rcopy(source.at[p] if each else source, dest.at[me], ssem.at[i], rsem.at[me], device(p)).start()
            return carry
        lax.fori_loop(1, 16, body, 0)

    def collect(source, dest, ssem, rsem, me, device, each, forward=None):
        if forward is not None:
            forward(me).start()

        def body(i, carry):
            p = lax.rem(me + i, 16)
            c = rcopy(source.at[p] if each else source, dest.at[p], ssem.at[i], rsem.at[p], device(p))
            c.wait_recv()
            if forward is not None:
                forward(p).start()
            c.wait_send()
            return carry
        lax.fori_loop(1, 16, body, 0)

    def to_partner(dest, ssem, rsem):
        return lambda p: rcopy(dest.at[core, p], dest.at[core, p], ssem.at[p], rsem.at[p], partner)

    def from_partner(dest, ssem, rsem):
        def body(p, carry):
            c = rcopy(dest.at[1 - core, p], dest.at[1 - core, p], ssem.at[p], rsem.at[p], partner)
            c.wait_recv()
            c.wait_send()
            return carry
        lax.fori_loop(0, 16, body, 0)

    def total(dest):
        acc = dest[0].astype(F32)
        for i in range(1, 16):
            acc = acc + dest[i].astype(F32)
        return acc

    mark("relayopp")
    relay_opposite()
    mark("fccwait")
    fcc.wait_recv()
    f16[...] = (fg[core] + fgp[...].astype(F32)).astype(BF16).reshape(16, 16, 512)
    f16r[slot] = f16[slot]
    spread(f16, f16r, s_f16, r_f16, slot, group, True)
    mark("relayside")
    relay_side()
    mark("relaylast")
    relay_last()

    mark("agwait")
    for g in range(4):
        ag_wait(g, far, 0)
        ag_wait(g, far, 1)
    for c in loads[8:10]:
        c.wait()
    mark("coarse")
    nall = ag[:, 0:16, :].reshape(256, D_C)
    call = ag[:, 16:32, :].reshape(256, D_C)
    proj = nt(cw[...], nall).astype(BF16)
    cqt, ckt, cvt = proj[0:64], proj[64:128], proj[128:192]
    cut = nt(cwo[...], call).astype(BF16)
    cs = tn(ckt, cqt) * scale
    ce = jnp.exp(cs - jnp.max(cs, axis=0, keepdims=True))
    cp = ce * (1.0 / jnp.sum(ce, axis=0, keepdims=True))
    cwt = cp.astype(BF16)
    cot = nn(cvt, cwt).astype(BF16)
    cdp = tn(cvt, cut)
    cdelta = jnp.sum(cp * cdp, axis=0, keepdims=True)
    cslope = (cp * (cdp - cdelta)).astype(BF16)
    cdt = jnp.concatenate(
        [nn(ckt, cslope) * scale, nt(cqt, cslope) * scale, nt(cut, cwt)], axis=0
    ).astype(BF16)
    mark("rs")
    rs_send[...] = tn(cdt, cw[...]).astype(BF16).reshape(4, 4, 16, D_C)
    rx = []
    for i in (1, 3, 2):
        x = lax.rem(gx + i, 4)
        c = rcopy(rs_send.at[x], rsx.at[i], s_rx.at[i], r_rx.at[i], (b, gy, x))
        c.start()
        rx.append(c)
    mark("cgrad")
    cgq = nn(cdt, nall)
    cgo = nn(cot, call)
    for half in range(2):
        lanes = slice(half * 512, (half + 1) * 512)
        cg[half, 0:192, :] = cgq[:, lanes]
        cg[half, 192:256, :] = cgo[:, lanes]
        cgb[half, 0:192, :] = cgq[:, lanes].astype(BF16)
        cgb[half, 192:256, :] = cgo[:, lanes].astype(BF16)
    cc = rcopy(cgb.at[1 - core], cgp, s_cc.at[0], r_cc.at[0], partner)
    cc.start()

    mark("f16wait")
    collect(f16, f16r, s_f16, r_f16, slot, group, True)
    fone[bz] = total(f16r).astype(BF16)
    spread(fone.at[bz], fone, s_f1, r_f1, bz, batch, False)

    mark("ccwait")
    cc.wait_recv()
    c16[...] = (cg[core] + cgp[...].astype(F32)).astype(BF16).reshape(16, 16, 512)
    c16r[bz] = c16[bz]
    spread(c16, c16r, s_c16, r_c16, bz, batch, True)

    mark("rsx")
    acc = rs_send[gx].astype(F32)
    for i, c in zip((1, 3, 2), rx):
        c.wait_recv()
        acc = acc + rsx[i].astype(F32)
    rsz_send[...] = acc.astype(BF16)
    rz = []
    for i in (1, 3, 2):
        g = lax.rem(gy + i, 4)
        c = rcopy(rsz_send.at[g], rsz.at[i], s_rz.at[i], r_rz.at[i], (b, g, gx))
        c.start()
        rz.append(c)

    mark("ghalowait")
    for c in ghalo:
        c.wait_recv()

    def owed(s):
        first, rows, cols = SEGMENTS[s][:3]
        return grecv[first - 256:first - 256 + rows * cols, :].astype(F32).reshape(rows, cols, 256)

    mark("dxf")
    dn[:, 0:8, :] += owed(LEFT)
    dn[:, 24:32, :] += owed(RIGHT)
    dn[0:3, :, :] += owed(TOP)
    dn[5:8, :, :] += owed(BOTTOM)
    dn[0:4, 0:8, :] += owed(TL)
    dn[0:4, 24:32, :] += owed(TR)
    dn[4:8, 0:8, :] += owed(BL)
    dn[4:8, 24:32, :] += owed(BR)
    xff = xf[...].astype(F32)
    inv_f = lax.rsqrt(jnp.mean(xff * xff, axis=-1, keepdims=True) + eps)
    dxf[...] = norm_backward(xff, inv_f, ff[...], dn[...].reshape(256, 256))

    mark("c16wait")
    collect(c16, c16r, s_c16, r_c16, bz, batch, True)
    cmine = cfin.at[core, bz]
    cmine[...] = total(c16r).astype(BF16)
    spread(cmine, cfin.at[core], s_cag, r_cag, bz, batch, False)

    mark("fonewait")
    collect(fone.at[bz], fone, s_f1, r_f1, bz, batch, False)
    fmine = ffin.at[core, slot]
    fmine[...] = total(fone).astype(BF16)
    spread(fmine, ffin.at[core], s_fag, r_fag, slot, group, False)

    mark("rszwait")
    dnc = rsz_send[gy].astype(F32)
    for i, c in zip((1, 3, 2), rz):
        c.wait_recv()
        dnc = dnc + rsz[i].astype(F32)
    xcf = xc[...]
    inv_c = lax.rsqrt(jnp.mean(xcf * xcf, axis=-1, keepdims=True) + eps)
    dxcv = norm_backward(xcf, inv_c, fc[...], dnc)
    for r in range(4):
        dxc[r] = dxcv[4 * r:4 * r + 4]

    mark("cagwait")
    collect(cmine, cfin.at[core], s_cag, r_cag, bz, batch, False, to_partner(cfin, s_cf, r_cf))
    mark("cfwait")
    from_partner(cfin, s_cf, r_cf)
    for half in range(2):
        lanes = slice(half * 512, (half + 1) * 512)
        done = cfin[half].reshape(256, 512)
        gcq[:, lanes] = done[0:192]
        gco[:, lanes] = done[192:256]

    mark("fagwait")
    collect(fmine, ffin.at[core], s_fag, r_fag, slot, group, False, to_partner(ffin, s_ff, r_ff))
    mark("ffwait")
    from_partner(ffin, s_ff, r_ff)
    gfq[:, 0:512] = ffin[0].reshape(256, 512)
    done = ffin[1].reshape(256, 512)
    gfq[:, 512:768] = done[:, 0:256]
    gfo[...] = done[:, 256:512]

    mark("sendwait")
    for c in sends + halo + ghalo + rx + rz + [cc, fcc]:
        c.wait_send()
    mark(None)


def writer(*refs):
    sems = refs[12]
    copies = [pltpu.make_async_copy(refs[i], refs[6 + i], sems.at[i]) for i in range(6)]
    for c in copies:
        c.start()
    for c in copies:
        c.wait()


def local(x_fine, dy_fine, x_coarse, dy_coarse, timestep, fine_gain, coarse_gain,
          fine_qkv, fine_out, coarse_qkv, coarse_out):
    vm = pl.BlockSpec(memory_space=pltpu.VMEM)
    hbm = pl.BlockSpec(memory_space=pltpu.HBM)
    dma = pltpu.SemaphoreType.DMA
    V = pltpu.VMEM
    outs = (
        jax.ShapeDtypeStruct((256, 256), BF16),
        jax.ShapeDtypeStruct((4, 4, D_C), BF16),
        jax.ShapeDtypeStruct((256, 768), BF16),
        jax.ShapeDtypeStruct((256, 256), BF16),
        jax.ShapeDtypeStruct((192, D_C), BF16),
        jax.ShapeDtypeStruct((64, D_C), BF16),
    )
    scratch = [
        V((256, 256), BF16), V((256, 256), BF16), V((4, 4, D_C), BF16), V((4, 4, D_C), BF16),
        V((1, 256), F32), V((1, D_C), F32), V((256, 768), BF16), V((256, 256), BF16),
        V((192, D_C), BF16), V((64, D_C), BF16), V((16, D_C), F32), V((1, 256), F32), V((1, D_C), F32),
        V((16, 32, D_C), BF16), V((KEYS, 256), BF16), V((KEYS, 512), BF16), V((2, 64, 256), BF16),
        V((KEYS, 256), F32), V((1024, 256), BF16), V((1024, 256), BF16),
        V((256, KEYS), BF16), V((256, KEYS), BF16), V((256, KEYS), BF16),
        V((KEYS, 1024), BF16), V((KEYS, 1024), BF16),
        V((256, 256), BF16), V((256, 256), F32), V((8, 32, 256), F32),
        V((HALO, 256), BF16), V((HALO, 256), BF16),
        V((4, 4, 16, D_C), BF16), V((4, 4, 16, D_C), BF16), V((4, 16, D_C), BF16), V((4, 16, D_C), BF16),
        V((2, 256, 512), F32), V((2, 256, 512), BF16), V((256, 512), BF16),
        V((16, 16, 512), BF16), V((16, 16, 512), BF16), V((2, 16, 16, 512), BF16),
        V((2, 256, 512), F32), V((2, 256, 512), BF16), V((256, 512), BF16),
        V((16, 16, 512), BF16), V((16, 16, 512), BF16), V((16, 16, 512), BF16), V((2, 16, 16, 512), BF16),
        dma((10,)), dma((24,)), dma((16, 2)), dma((8,)), dma((8,)), dma((8,)), dma((8,)),
        dma((4,)), dma((4,)), dma((4,)), dma((4,)),
        dma((2,)), dma((2,)), dma((16,)), dma((16,)), dma((16,)), dma((16,)), dma((16,)), dma((16,)),
        dma((2,)), dma((2,)), dma((16,)), dma((16,)), dma((16,)), dma((16,)), dma((16,)), dma((16,)),
        dma((16,)), dma((16,)),
    ]
    results = pl.pallas_call(
        kernel,
        out_shape=outs,
        in_specs=[pl.BlockSpec(memory_space=pltpu.SMEM)] + [hbm] * 10,
        out_specs=[vm] * 6,
        scratch_shapes=scratch,
        compiler_params=pltpu.CompilerParams(
            collective_id=0, has_side_effects=True, vmem_limit_bytes=50 * 1024 * 1024
        ),
    )(timestep, *[
        pltpu.with_memory_space_constraint(a, pltpu.HBM) for a in (
            x_fine.reshape(256, D_F), dy_fine.reshape(256, D_F),
            x_coarse.reshape(4, 4, D_C), dy_coarse.reshape(4, 4, D_C),
            fine_gain[None], coarse_gain[None],
            fine_qkv, fine_out, coarse_qkv.reshape(192, D_C), coarse_out,
        )
    ])
    dxf, dxc, gfq, gfo, gcq, gco = pl.pallas_call(
        writer,
        out_shape=tuple(pltpu.HBM(o.shape, o.dtype) for o in outs),
        in_specs=[vm] * 6,
        out_specs=[hbm] * 6,
        scratch_shapes=[dma((6,))],
    )(*[pltpu.with_memory_space_constraint(r, pltpu.VMEM) for r in results])
    return (
        dxf.reshape(x_fine.shape),
        dxc.reshape(x_coarse.shape),
        gfq,
        gfo,
        gcq.reshape(coarse_qkv.shape),
        gco,
    )


def solution(mesh):
    tile = P("batch", "gy", "gx", None)
    heads = P(None, ("gy", "gx"), None)
    rows = P(("gy", "gx"), None)
    return jax.shard_map(
        local,
        mesh=mesh,
        in_specs=(tile, tile, tile, tile, P("batch"), P(), P(), P(), P(), heads, rows),
        out_specs=(tile, tile, P(), P(), heads, rows),
        check_vma=False,
    )
```

time: 97.5 us -> 72.6 us (0.74)
  Pallas kernels: 83.9 us -> 71.2 us
  local copies, waits for them, and re-layouts: 10.3 us -> 0 us
  other arithmetic: 1.48 us -> 0 us
    pallas_call x1 -> x2, Pallas kernels: 83.9 us -> 71.2 us  [the longest x1 70.1 us: local(): pl.pallas_call(kernel, out_shape=outs, in_specs=[pl.BlockSpec(memory_spac...]
    unnamed x17 -> x0, local copies, waits for them, and re-layouts: 8.16 us -> none
    reshape x3 -> x0, local copies, waits for them, and re-layouts: 2.18 us -> none  [the longest x1 0.78 us: local(): x_coarse.reshape(16, D_C)]
    mul x2 -> x0, other arithmetic: 1.48 us -> none  [time_gain(): return gains * (1.0 + 0.5 * jnp.cos(step_value.astype(F32) * frequency))]
where the time goes in v2:
time: 72.6 us; the launch traced here: 72.5 us
  Pallas kernels  71.2 us (98%)
  between operations  1.29 us (2%)
    pallas_call x1, Pallas kernels, local(): pl.pallas_call(kernel, out_shape=outs, in_specs=[pl.BlockSpec(memory_spac...  70.1 us

profile of v2, /device:TPU:1, one launch (start us, length us, event | category | flops | bytes accessed | tf_op | source)
XLA Modules:
  0.0 72.5 jit_solution(332013573882951575)
XLA Ops:
  1.3 70.1 %shard_map.154 = (bf16[256,256]{1,0:T(8,128)(2,1)S(1)}, bf16[4,4,1024]{2,1,0:T(4,128)(2,1)S(1)}, bf16[256,768]{1,0:T(8,128)(2,1)S(1)}, bf16[256,256]{1,0:T(8,128...) custom-call(s32[1]{0:T(128)S(6)} %copy.17.t_ref, bf16[256,256]{1,0:T(8,128)(2,1)} %bitcast.11, ...), custom_call_target="tpu_custom_call" | custom-call | tf_op jit(solution)/shard_map/pallas_call | solution.py:552
  71.4 1.1 %shard_map.155 = (bf16[256,256]{1,0:T(8,128)(2,1)}, bf16[4,4,1024]{2,1,0:T(4,128)(2,1)}, bf16[256,768]{1,0:T(8,128)(2,1)}, bf16[256,256]{1,0:T(8,128)(2,1)}, bf1...) custom-call(bf16[256,256]{1,0:T(8,128)(2,1)S(1)} %get-tuple-element.18.refs_0_, ...), custom_call_target="tpu_custom_call" | custom-call | tf_op jit(solution)/shard_map/pallas_call | solution.py:569

commit v3 on v2

--- a/solution.py
+++ b/solution.py
@@ -23,16 +23,16 @@
 OWN, LEFT, RIGHT, TOP, BOTTOM, TL, TR, BL, BR = range(9)
 SEGMENTS = (
     (0, 8, 32, 0, 0),
-    (256, 8, 8, 0, -8),
-    (320, 8, 8, 0, 32),
-    (384, 3, 32, -3, 0),
-    (480, 3, 32, 8, 0),
-    (576, 4, 8, -4, -8),
-    (608, 4, 8, -4, 32),
-    (640, 4, 8, 8, -8),
-    (672, 4, 8, 8, 32),
+    (256, 8, 4, 0, -4),
+    (288, 8, 4, 0, 32),
+    (320, 3, 32, -3, 0),
+    (416, 3, 32, 8, 0),
+    (512, 4, 4, -4, -4),
+    (528, 4, 4, -4, 32),
+    (544, 4, 4, 8, -4),
+    (560, 4, 4, 8, 32),
 )
-KEYS = 704
+KEYS = 576
 HALO = KEYS - 256
 FROM = {LEFT: (0, -1), RIGHT: (0, 1), TOP: (-1, 0), BOTTOM: (1, 0),
         TL: (-1, -1), TR: (-1, 1), BL: (1, -1), BR: (1, 1)}
@@ -80,13 +80,13 @@
     t_ref, xf_h, dyf_h, xc_h, dyc_h, gf_h, gc_h, wqkv_h, wout_h, cw_h, cwo_h,
     dxf, dxc, gfq, gfo, gcq, gco,
     xf, dyf, xc4, dyc4, gf, gc, wqkv, wout, cw, cwo, xc, ff, fc,
-    ag, nrm, kv, edge, bias, qm, um, kt, vt, nt_all, wall, sall, att, dqt, dn, gsend, grecv,
+    ag, nrm, kv, edge32, edge, bias, qm, um, kt, vt, nt_all, wall, sall, att, dqt, dn, gsend, grecv,
     rs_send, rsx, rsz_send, rsz,
     cg, cgb, cgp, c16, c16r, cfin,
-    fg, fgb, fgp, f16, f16r, fone, ffin,
+    fg, fgb, fgp, fxs, fxr, fzs, fzr, fyr, ffin,
     s_in, s_ag, r_ag, s_h, r_h, s_g, r_g, s_rx, r_rx, s_rz, r_rz,
     s_cc, r_cc, s_c16, r_c16, s_cag, r_cag, s_cf, r_cf,
-    s_fc, r_fc, s_f16, r_f16, s_f1, r_f1, s_fag, r_fag, s_ff, r_ff,
+    s_fc, r_fc, s_fx, r_fx, s_fz, r_fz, s_fy, r_fy, s_fzg, r_fzg, s_fxg, r_fxg, s_ff, r_ff,
 ):
     b = lax.axis_index("batch")
     gy = lax.axis_index("gy")
@@ -102,6 +102,16 @@
         return (p * 2 + core, gy, gx)
 
     partner = (b + 1 - 2 * core, gy, gx)
+
+    zlo = b // 16
+    yy = lax.rem(bz, 8)
+    zz = gy * 2 + zlo
+
+    def along_z(p):
+        return (lax.rem(p, 2) * 16 + yy * 2 + core, p // 2, gx)
+
+    def along_y(p):
+        return (zlo * 16 + p * 2 + core, gy, gx)
 
     mark("greet")
     loads = [
@@ -122,6 +132,9 @@
 
     lax.fori_loop(1, 16, greet, 0)
     pl.semaphore_signal(barrier, inc=1, device_id=partner, device_id_type=MESH)
+    for i in (1, 2, 3):
+        other = along_z(lax.rem(gy + i, 4) * 2 + 1 - zlo)
+        pl.semaphore_signal(barrier, inc=1, device_id=other, device_id_type=MESH)
 
     mark("norms")
     step_value = t_ref[0].astype(F32)
@@ -136,8 +149,10 @@
     normed = normf.astype(BF16)
     nrm[0:256, :] = normed
     norm3 = normf.reshape(8, 32, 256)
-    edge[0, :, :] = norm3[:, 0:8, :].reshape(64, 256).astype(BF16)
-    edge[1, :, :] = norm3[:, 24:32, :].reshape(64, 256).astype(BF16)
+    for r in range(8):
+        edge32[0, 4 * r:4 * r + 4, :] = norm3[r, 0:4, :]
+        edge32[1, 4 * r:4 * r + 4, :] = norm3[r, 28:32, :]
+    edge[...] = edge32[...].astype(BF16)
 
     for c in loads[3:5]:
         c.wait()
@@ -149,14 +164,14 @@
     ag[slot, 16:32, :] = jnp.concatenate([dyc4[r].astype(F32) for r in range(4)], axis=0).astype(BF16)
 
     mark("barwait")
-    pl.semaphore_wait(barrier, 31)
+    pl.semaphore_wait(barrier, 34)
 
     mark("send0")
     src = {
         LEFT: edge.at[1], RIGHT: edge.at[0],
         TOP: nrm.at[pl.ds(160, 96)], BOTTOM: nrm.at[pl.ds(0, 96)],
-        TL: edge.at[1, pl.ds(32, 32)], TR: edge.at[0, pl.ds(32, 32)],
-        BL: edge.at[1, pl.ds(0, 32)], BR: edge.at[0, pl.ds(0, 32)],
+        TL: edge.at[1, pl.ds(16, 16)], TR: edge.at[0, pl.ds(16, 16)],
+        BL: edge.at[1, pl.ds(0, 16)], BR: edge.at[0, pl.ds(0, 16)],
     }
 
     def toward(step):
@@ -173,28 +188,27 @@
 
     up, down, opp = lax.rem(gy + 1, 4), lax.rem(gy + 3, 4), lax.rem(gy + 2, 4)
     right, left, far = lax.rem(gx + 1, 4), lax.rem(gx + 3, 4), lax.rem(gx + 2, 4)
-    to_up, to_down = (b, up, gx), (b, down, gx)
-    to_right, to_left = (b, gy, right), (b, gy, left)
     sends = []
 
-    def ag_send(g, x, part, device):
+    def ag_copy(g, x, part, device):
         sl = x * 4 + g
         block = ag.at[sl] if part is None else ag.at[sl, pl.ds(16 * part, 16)]
-        c = rcopy(block, block, s_ag.at[len(sends)], r_ag.at[sl, part or 0], device)
+        return rcopy(block, block, s_ag.at[len(sends)], r_ag.at[sl, part or 0], device)
+
+    def ag_send(g, x, device, part=None):
+        c = ag_copy(g, x, part, device)
         c.start()
         sends.append(c)
 
     def ag_wait(g, x, part=None):
-        sl = x * 4 + g
-        block = ag.at[sl] if part is None else ag.at[sl, pl.ds(16 * part, 16)]
-        rcopy(block, block, s_ag.at[0], r_ag.at[sl, part or 0], to_up).wait_recv()
-
+        ag_copy(g, x, part, partner).wait_recv()
+
+    for g in (up, down):
+        ag_send(gy, gx, (b, g, gx))
+    for x in (far, right, left):
+        ag_send(gy, gx, (b, gy, x))
     for s in (TL, TR, BL, BR, TOP, BOTTOM, LEFT, RIGHT):
         halo[s - 1].start()
-    ag_send(gy, gx, None, to_up)
-    ag_send(gy, gx, None, to_down)
-    ag_send(gy, gx, None, to_right)
-    ag_send(gy, gx, None, to_left)
 
     mark("qmask")
     for c in loads[5:8]:
@@ -221,38 +235,12 @@
             floor = jnp.minimum(floor, jnp.where(ok_side[s], 0.0, -1e30).astype(F32))
         bias[first:first + n, :] = floor
 
-    def relay_near():
-        ag_wait(gy, left)
-        ag_send(gy, left, 0, to_right)
-        ag_wait(gy, right)
-        ag_send(gy, right, 1, to_left)
-        ag_wait(down, gx)
-        ag_send(down, gx, 0, to_up)
-        ag_send(down, gx, None, to_right)
-        ag_send(down, gx, None, to_left)
-        ag_wait(up, gx)
-        ag_send(up, gx, 1, to_down)
-        ag_send(up, gx, None, to_right)
-        ag_send(up, gx, None, to_left)
-
-    def relay_opposite():
-        ag_wait(opp, gx, 0)
-        ag_wait(opp, gx, 1)
-        ag_send(opp, gx, None, to_right)
-        ag_send(opp, gx, None, to_left)
-
-    def relay_side():
-        for g in (down, up):
-            ag_wait(g, left)
-            ag_send(g, left, 0, to_right)
-            ag_wait(g, right)
-            ag_send(g, right, 1, to_left)
-
-    def relay_last():
-        ag_wait(opp, left)
-        ag_send(opp, left, 0, to_right)
-        ag_wait(opp, right)
-        ag_send(opp, right, 1, to_left)
+    mark("forward")
+    for g, part, device in ((down, 0, (b, up, gx)), (up, 1, (b, down, gx))):
+        ag_wait(g, gx)
+        ag_send(g, gx, device, part)
+        for x in (far, right, left):
+            ag_send(g, gx, (b, gy, x))
 
     mark("halowait")
     for c in halo:
@@ -282,8 +270,11 @@
     mark("head01")
     head(0)
     head(1)
-    mark("relaynear")
-    relay_near()
+    mark("forward2")
+    ag_wait(opp, gx, 0)
+    ag_wait(opp, gx, 1)
+    for x in (far, right, left):
+        ag_send(opp, gx, (b, gy, x))
     mark("head23")
     head(2)
     head(3)
@@ -319,60 +310,57 @@
         nt(dq, wqkv[:, 0:256]) + nt(dk[0:256], wqkv[:, 256:512]) + nt(dv[0:256], wqkv[:, 512:768])
     ).reshape(8, 32, 256)
 
-    def spread(source, dest, ssem, rsem, me, device, each):
+    def spread(source, dest, ssem, rsem, me, device, each, n=16):
         def body(i, carry):
-            p = lax.rem(me + i, 16)
+            p = lax.rem(me + i, n)
             rcopy(source.at[p] if each else source, dest.at[me], ssem.at[i], rsem.at[me], device(p)).start()
             return carry
-        lax.fori_loop(1, 16, body, 0)
-
-    def collect(source, dest, ssem, rsem, me, device, each, forward=None):
+        lax.fori_loop(1, n, body, 0)
+
+    def collect(source, dest, ssem, rsem, me, device, each, forward=None, n=16):
         if forward is not None:
             forward(me).start()
 
         def body(i, carry):
-            p = lax.rem(me + i, 16)
+            p = lax.rem(me + i, n)
             c = rcopy(source.at[p] if each else source, dest.at[p], ssem.at[i], rsem.at[p], device(p))
             c.wait_recv()
             if forward is not None:
                 forward(p).start()
             c.wait_send()
             return carry
-        lax.fori_loop(1, 16, body, 0)
+        lax.fori_loop(1, n, body, 0)
 
     def to_partner(dest, ssem, rsem):
         return lambda p: rcopy(dest.at[core, p], dest.at[core, p], ssem.at[p], rsem.at[p], partner)
 
-    def from_partner(dest, ssem, rsem):
+    def from_partner(dest, ssem, rsem, n=16):
         def body(p, carry):
             c = rcopy(dest.at[1 - core, p], dest.at[1 - core, p], ssem.at[p], rsem.at[p], partner)
             c.wait_recv()
             c.wait_send()
             return carry
-        lax.fori_loop(0, 16, body, 0)
-
-    def total(dest):
+        lax.fori_loop(0, n, body, 0)
+
+    def total(dest, n=16):
         acc = dest[0].astype(F32)
-        for i in range(1, 16):
+        for i in range(1, n):
             acc = acc + dest[i].astype(F32)
         return acc
 
-    mark("relayopp")
-    relay_opposite()
     mark("fccwait")
     fcc.wait_recv()
-    f16[...] = (fg[core] + fgp[...].astype(F32)).astype(BF16).reshape(16, 16, 512)
-    f16r[slot] = f16[slot]
-    spread(f16, f16r, s_f16, r_f16, slot, group, True)
-    mark("relayside")
-    relay_side()
-    mark("relaylast")
-    relay_last()
-
+    fxs[...] = (fg[core] + fgp[...].astype(F32)).astype(BF16).reshape(4, 64, 512)
+    fx = []
+    for i in (1, 3, 2):
+        x = lax.rem(gx + i, 4)
+        c = rcopy(fxs.at[x], fxr.at[i], s_fx.at[i], r_fx.at[i], (b, gy, x))
+        c.start()
+        fx.append(c)
     mark("agwait")
-    for g in range(4):
-        ag_wait(g, far, 0)
-        ag_wait(g, far, 1)
+    for g in (gy, down, up, opp):
+        for x in (right, left, far):
+            ag_wait(g, x)
     for c in loads[8:10]:
         c.wait()
     mark("coarse")
@@ -412,16 +400,26 @@
     cc = rcopy(cgb.at[1 - core], cgp, s_cc.at[0], r_cc.at[0], partner)
     cc.start()
 
-    mark("f16wait")
-    collect(f16, f16r, s_f16, r_f16, slot, group, True)
-    fone[bz] = total(f16r).astype(BF16)
-    spread(fone.at[bz], fone, s_f1, r_f1, bz, batch, False)
+    mark("fxwait")
+    acc = fxs[gx].astype(F32)
+    for i, c in zip((1, 3, 2), fx):
+        c.wait_recv()
+        acc = acc + fxr[i].astype(F32)
+    for j in range(2):
+        fzs[4 * j:4 * j + 4] = acc[:, 256 * j:256 * (j + 1)].astype(BF16).reshape(4, 16, 256)
+    fzr[zz] = fzs[zz]
+    spread(fzs, fzr, s_fz, r_fz, zz, along_z, True, n=8)
 
     mark("ccwait")
     cc.wait_recv()
     c16[...] = (cg[core] + cgp[...].astype(F32)).astype(BF16).reshape(16, 16, 512)
     c16r[bz] = c16[bz]
     spread(c16, c16r, s_c16, r_c16, bz, batch, True)
+
+    mark("fzwait")
+    collect(fzs, fzr, s_fz, r_fz, zz, along_z, True, n=8)
+    fyr[yy] = total(fzr, 8).astype(BF16)
+    spread(fyr.at[yy], fyr, s_fy, r_fy, yy, along_y, False, n=8)
 
     mark("rsx")
     acc = rs_send[gx].astype(F32)
@@ -445,29 +443,28 @@
         return grecv[first - 256:first - 256 + rows * cols, :].astype(F32).reshape(rows, cols, 256)
 
     mark("dxf")
-    dn[:, 0:8, :] += owed(LEFT)
-    dn[:, 24:32, :] += owed(RIGHT)
     dn[0:3, :, :] += owed(TOP)
     dn[5:8, :, :] += owed(BOTTOM)
-    dn[0:4, 0:8, :] += owed(TL)
-    dn[0:4, 24:32, :] += owed(TR)
-    dn[4:8, 0:8, :] += owed(BL)
-    dn[4:8, 24:32, :] += owed(BR)
+    for s, row0, col0 in ((LEFT, 0, 0), (RIGHT, 0, 28), (TL, 0, 0), (TR, 0, 28), (BL, 4, 0), (BR, 4, 28)):
+        share = owed(s)
+        for r in range(SEGMENTS[s][1]):
+            dn[row0 + r, col0:col0 + 4, :] += share[r]
     xff = xf[...].astype(F32)
     inv_f = lax.rsqrt(jnp.mean(xff * xff, axis=-1, keepdims=True) + eps)
     dxf[...] = norm_backward(xff, inv_f, ff[...], dn[...].reshape(256, 256))
+
+    mark("fywait")
+    collect(fyr.at[yy], fyr, s_fy, r_fy, yy, along_y, False, n=8)
+    fcol = ffin.at[core, gx]
+    fmine = fcol.at[zz]
+    fmine[...] = total(fyr, 8).astype(BF16)
+    spread(fmine, fcol, s_fzg, r_fzg, zz, along_z, False, n=8)
 
     mark("c16wait")
     collect(c16, c16r, s_c16, r_c16, bz, batch, True)
     cmine = cfin.at[core, bz]
     cmine[...] = total(c16r).astype(BF16)
     spread(cmine, cfin.at[core], s_cag, r_cag, bz, batch, False)
-
-    mark("fonewait")
-    collect(fone.at[bz], fone, s_f1, r_f1, bz, batch, False)
-    fmine = ffin.at[core, slot]
-    fmine[...] = total(fone).astype(BF16)
-    spread(fmine, ffin.at[core], s_fag, r_fag, slot, group, False)
 
     mark("rszwait")
     dnc = rsz_send[gy].astype(F32)
@@ -480,6 +477,10 @@
     for r in range(4):
         dxc[r] = dxcv[4 * r:4 * r + 4]
 
+    mark("fzgwait")
+    collect(fmine, fcol, s_fzg, r_fzg, zz, along_z, False, n=8)
+    spread(fcol, ffin.at[core], s_fxg, r_fxg, gx, lambda p: (b, gy, p), False, n=4)
+
     mark("cagwait")
     collect(cmine, cfin.at[core], s_cag, r_cag, bz, batch, False, to_partner(cfin, s_cf, r_cf))
     mark("cfwait")
@@ -490,17 +491,19 @@
         gcq[:, lanes] = done[0:192]
         gco[:, lanes] = done[192:256]
 
-    mark("fagwait")
-    collect(fmine, ffin.at[core], s_fag, r_fag, slot, group, False, to_partner(ffin, s_ff, r_ff))
+    mark("fxgwait")
+    collect(fcol, ffin.at[core], s_fxg, r_fxg, gx, lambda p: (b, gy, p), False, to_partner(ffin, s_ff, r_ff), n=4)
     mark("ffwait")
-    from_partner(ffin, s_ff, r_ff)
-    gfq[:, 0:512] = ffin[0].reshape(256, 512)
-    done = ffin[1].reshape(256, 512)
-    gfq[:, 512:768] = done[:, 0:256]
-    gfo[...] = done[:, 256:512]
+    from_partner(ffin, s_ff, r_ff, n=4)
+    for x in range(4):
+        rows = slice(64 * x, 64 * (x + 1))
+        quarter = [ffin[half, x, 4 * j:4 * j + 4].reshape(64, 256) for half in range(2) for j in range(2)]
+        for i in range(3):
+            gfq[rows, 256 * i:256 * (i + 1)] = quarter[i]
+        gfo[rows, :] = quarter[3]
 
     mark("sendwait")
-    for c in sends + halo + ghalo + rx + rz + [cc, fcc]:
+    for c in sends + halo + ghalo + rx + rz + fx + [cc, fcc]:
         c.wait_send()
     mark(None)
 
@@ -532,7 +535,7 @@
         V((256, 256), BF16), V((256, 256), BF16), V((4, 4, D_C), BF16), V((4, 4, D_C), BF16),
         V((1, 256), F32), V((1, D_C), F32), V((256, 768), BF16), V((256, 256), BF16),
         V((192, D_C), BF16), V((64, D_C), BF16), V((16, D_C), F32), V((1, 256), F32), V((1, D_C), F32),
-        V((16, 32, D_C), BF16), V((KEYS, 256), BF16), V((KEYS, 512), BF16), V((2, 64, 256), BF16),
+        V((16, 32, D_C), BF16), V((KEYS, 256), BF16), V((KEYS, 512), BF16), V((2, 32, 256), F32), V((2, 32, 256), BF16),
         V((KEYS, 256), F32), V((1024, 256), BF16), V((1024, 256), BF16),
         V((256, KEYS), BF16), V((256, KEYS), BF16), V((256, KEYS), BF16),
         V((KEYS, 1024), BF16), V((KEYS, 1024), BF16),
@@ -542,12 +545,13 @@
         V((2, 256, 512), F32), V((2, 256, 512), BF16), V((256, 512), BF16),
         V((16, 16, 512), BF16), V((16, 16, 512), BF16), V((2, 16, 16, 512), BF16),
         V((2, 256, 512), F32), V((2, 256, 512), BF16), V((256, 512), BF16),
-        V((16, 16, 512), BF16), V((16, 16, 512), BF16), V((16, 16, 512), BF16), V((2, 16, 16, 512), BF16),
-        dma((10,)), dma((24,)), dma((16, 2)), dma((8,)), dma((8,)), dma((8,)), dma((8,)),
+        V((4, 64, 512), BF16), V((4, 64, 512), BF16), V((8, 16, 256), BF16), V((8, 16, 256), BF16),
+        V((8, 16, 256), BF16), V((2, 4, 8, 16, 256), BF16),
+        dma((10,)), dma((16,)), dma((16, 2)), dma((8,)), dma((8,)), dma((8,)), dma((8,)),
         dma((4,)), dma((4,)), dma((4,)), dma((4,)),
         dma((2,)), dma((2,)), dma((16,)), dma((16,)), dma((16,)), dma((16,)), dma((16,)), dma((16,)),
-        dma((2,)), dma((2,)), dma((16,)), dma((16,)), dma((16,)), dma((16,)), dma((16,)), dma((16,)),
-        dma((16,)), dma((16,)),
+        dma((2,)), dma((2,)), dma((4,)), dma((4,)), dma((8,)), dma((8,)), dma((8,)), dma((8,)),
+        dma((8,)), dma((8,)), dma((4,)), dma((4,)), dma((4,)), dma((4,)),
     ]
     results = pl.pallas_call(
         kernel,

time: 72.6 us -> 65.7 us (0.905)
  Pallas kernels: 71.2 us -> 64.3 us
    pallas_call x1, Pallas kernels: 70.1 us -> 63.2 us  [local(): pl.pallas_call(kernel, out_shape=outs, in_specs=[pl.BlockSpec(memory_spac...]
where the time goes in v3:
time: 65.7 us; the launch traced here: 65.5 us
  Pallas kernels  64.3 us (98%)
  between operations  1.29 us (2%)
    pallas_call x1, Pallas kernels, local(): pl.pallas_call(kernel, out_shape=outs, in_specs=[pl.BlockSpec(memory_spac...  63.2 us

profile of v3, /device:TPU:1, one launch (start us, length us, event | category | flops | bytes accessed | tf_op | source)
XLA Modules:
  0.0 65.5 jit_solution(10145815214935634590)
XLA Ops:
  1.3 63.2 %shard_map.154 = (bf16[256,256]{1,0:T(8,128)(2,1)S(1)}, bf16[4,4,1024]{2,1,0:T(4,128)(2,1)S(1)}, bf16[256,768]{1,0:T(8,128)(2,1)S(1)}, bf16[256,256]{1,0:T(8,128...) custom-call(s32[1]{0:T(128)S(6)} %copy.17.t_ref, bf16[256,256]{1,0:T(8,128)(2,1)} %bitcast.11, ...), custom_call_target="tpu_custom_call" | custom-call | tf_op jit(solution)/shard_map/pallas_call | solution.py:556
  64.5 1.1 %shard_map.155 = (bf16[256,256]{1,0:T(8,128)(2,1)}, bf16[4,4,1024]{2,1,0:T(4,128)(2,1)}, bf16[256,768]{1,0:T(8,128)(2,1)}, bf16[256,256]{1,0:T(8,128)(2,1)}, bf1...) custom-call(bf16[256,256]{1,0:T(8,128)(2,1)S(1)} %get-tuple-element.18.refs_0_, ...), custom_call_target="tpu_custom_call" | custom-call | tf_op jit(solution)/shard_map/pallas_call | solution.py:573

commit v4 on v3

--- a/solution.py
+++ b/solution.py
@@ -62,6 +62,10 @@
     )
 
 
+def drain(ref, sem):
+    pltpu.make_async_copy(ref, ref, sem).wait()
+
+
 def time_gain(gains, step_value):
     channels = gains.shape[1]
     place = lax.broadcasted_iota(jnp.int32, (8, channels), 1).astype(F32)
@@ -80,11 +84,11 @@
     t_ref, xf_h, dyf_h, xc_h, dyc_h, gf_h, gc_h, wqkv_h, wout_h, cw_h, cwo_h,
     dxf, dxc, gfq, gfo, gcq, gco,
     xf, dyf, xc4, dyc4, gf, gc, wqkv, wout, cw, cwo, xc, ff, fc,
-    ag, nrm, kv, edge32, edge, bias, qm, um, kt, vt, nt_all, wall, sall, att, dqt, dn, gsend, grecv,
+    ag, nrm, kv, edge32, edge, bias, qm, um, kt, vt, nt_all, wall, sall, oexp, odp, otop, osum, odel, att, dqt, dn, gsend, grecv,
     rs_send, rsx, rsz_send, rsz,
     cg, cgb, cgp, c16, c16r, cfin,
     fg, fgb, fgp, fxs, fxr, fzs, fzr, fyr, ffin,
-    s_in, s_ag, r_ag, s_h, r_h, s_g, r_g, s_rx, r_rx, s_rz, r_rz,
+    heard, s_in, s_ag, r_ag, s_h, r_h, s_g, r_g, s_rx, r_rx, s_rz, r_rz,
     s_cc, r_cc, s_c16, r_c16, s_cag, r_cag, s_cf, r_cf,
     s_fc, r_fc, s_fx, r_fx, s_fz, r_fz, s_fy, r_fy, s_fzg, r_fzg, s_fxg, r_fxg, s_ff, r_ff,
 ):
@@ -109,6 +113,9 @@
 
     def along_z(p):
         return (lax.rem(p, 2) * 16 + yy * 2 + core, p // 2, gx)
+
+    def along_x(p):
+        return (b, gy, p)
 
     def along_y(p):
         return (zlo * 16 + p * 2 + core, gy, gx)
@@ -125,16 +132,17 @@
         c.start()
     barrier = pltpu.get_barrier_semaphore()
 
-    def greet(i, carry):
-        pl.semaphore_signal(barrier, inc=1, device_id=group(lax.rem(slot + i, 16)), device_id_type=MESH)
-        pl.semaphore_signal(barrier, inc=1, device_id=batch(lax.rem(bz + i, 16)), device_id_type=MESH)
-        return carry
-
-    lax.fori_loop(1, 16, greet, 0)
-    pl.semaphore_signal(barrier, inc=1, device_id=partner, device_id_type=MESH)
-    for i in (1, 2, 3):
-        other = along_z(lax.rem(gy + i, 4) * 2 + 1 - zlo)
-        pl.semaphore_signal(barrier, inc=1, device_id=other, device_id_type=MESH)
+    def toward(step):
+        return (b, lax.rem(gy + step[0] + 4, 4), lax.rem(gx + step[1] + 4, 4))
+
+    near = [toward(FROM[s]) for s in range(1, 9)]
+    line = [along_y(lax.rem(yy + 1, 8)), along_y(lax.rem(yy + 7, 8)), (b + 16 - 32 * zlo, gy, gx)]
+
+    def tell(sem, devices):
+        for device in devices:
+            pl.semaphore_signal(sem, inc=1, device_id=device, device_id_type=MESH)
+
+    tell(barrier, near + line + [partner])
 
     mark("norms")
     step_value = t_ref[0].astype(F32)
@@ -164,7 +172,7 @@
     ag[slot, 16:32, :] = jnp.concatenate([dyc4[r].astype(F32) for r in range(4)], axis=0).astype(BF16)
 
     mark("barwait")
-    pl.semaphore_wait(barrier, 34)
+    pl.semaphore_wait(barrier, 12)
 
     mark("send0")
     src = {
@@ -174,42 +182,32 @@
         BL: edge.at[1, pl.ds(0, 16)], BR: edge.at[0, pl.ds(0, 16)],
     }
 
-    def toward(step):
-        return (b, lax.rem(gy + step[0] + 4, 4), lax.rem(gx + step[1] + 4, 4))
-
     def size(s):
         return SEGMENTS[s][1] * SEGMENTS[s][2]
 
     halo = []
     for s in range(1, 9):
         dy, dx = FROM[s]
-        halo.append(rcopy(src[s], nrm.at[pl.ds(SEGMENTS[s][0], size(s))], s_h.at[s - 1], r_h.at[s - 1],
+        halo.append(rcopy(src[s], nrm.at[pl.ds(SEGMENTS[s][0], size(s))], s_h, r_h,
                           toward((-dy, -dx))))
 
     up, down, opp = lax.rem(gy + 1, 4), lax.rem(gy + 3, 4), lax.rem(gy + 2, 4)
     right, left, far = lax.rem(gx + 1, 4), lax.rem(gx + 3, 4), lax.rem(gx + 2, 4)
-    sends = []
-
-    def ag_copy(g, x, part, device):
+    NEAR, OPP, REST = 0, 2, 3
+
+    def ag_send(g, x, device, arrival, part=None):
         sl = x * 4 + g
         block = ag.at[sl] if part is None else ag.at[sl, pl.ds(16 * part, 16)]
-        return rcopy(block, block, s_ag.at[len(sends)], r_ag.at[sl, part or 0], device)
-
-    def ag_send(g, x, device, part=None):
-        c = ag_copy(g, x, part, device)
-        c.start()
-        sends.append(c)
-
-    def ag_wait(g, x, part=None):
-        ag_copy(g, x, part, partner).wait_recv()
-
-    for g in (up, down):
-        ag_send(gy, gx, (b, g, gx))
-    for x in (far, right, left):
-        ag_send(gy, gx, (b, gy, x))
+        rcopy(block, block, s_ag, r_ag.at[arrival], device).start()
+
+    for i, g in enumerate((up, down)):
+        ag_send(gy, gx, (b, g, gx), NEAR + i)
+    for x in (right, left):
+        ag_send(gy, gx, (b, gy, x), REST)
+
     for s in (TL, TR, BL, BR, TOP, BOTTOM, LEFT, RIGHT):
         halo[s - 1].start()
-
+    tell(heard.at[0], near + line)
     mark("qmask")
     for c in loads[5:8]:
         c.wait()
@@ -235,52 +233,79 @@
             floor = jnp.minimum(floor, jnp.where(ok_side[s], 0.0, -1e30).astype(F32))
         bias[first:first + n, :] = floor
 
+    mark("own")
+    kt[:, 0:256] = kv[0:256, 0:256].T
+    vt[:, 0:256] = kv[0:256, 256:512].T
+    nt_all[:, 0:256] = nrm[0:256, :].T
+    for h in range(H_F):
+        heads = slice(h * 256, (h + 1) * 256)
+        s = nt(kv[0:256, 0:256], qm[heads, :]) * scale + bias[0:256, :]
+        top = jnp.max(s, axis=0, keepdims=True)
+        e = jnp.exp(s - top)
+        dp = nt(kv[0:256, 256:512], um[heads, :])
+        oexp[:, heads] = e
+        odp[:, heads] = dp
+        otop[h:h + 1, :] = top
+        osum[h:h + 1, :] = jnp.sum(e, axis=0, keepdims=True)
+        odel[h:h + 1, :] = jnp.sum(e * dp, axis=0, keepdims=True)
+
+    mark("heard0")
+    pl.semaphore_wait(heard.at[0], 11)
+    tell(heard.at[1], line)
+    ag_send(gy, gx, (b, gy, far), REST)
     mark("forward")
-    for g, part, device in ((down, 0, (b, up, gx)), (up, 1, (b, down, gx))):
-        ag_wait(g, gx)
-        ag_send(g, gx, device, part)
+    for i, (g, device) in enumerate(((down, (b, up, gx)), (up, (b, down, gx)))):
+        drain(ag.at[0], r_ag.at[NEAR + i])
+        ag_send(g, gx, device, OPP, i)
         for x in (far, right, left):
-            ag_send(g, gx, (b, gy, x))
+            ag_send(g, gx, (b, gy, x), REST)
 
     mark("halowait")
-    for c in halo:
-        c.wait_recv()
+    drain(nrm.at[pl.ds(256, HALO)], r_h)
 
     mark("transp")
+    pl.semaphore_wait(heard.at[1], 3)
+    tell(heard.at[2], line)
     kv[256:KEYS, :] = nn(nrm[256:KEYS, :], wqkv[:, 256:768]).astype(BF16)
-    kt[...] = kv[:, 0:256].T
-    vt[...] = kv[:, 256:512].T
+    kt[:, 256:KEYS] = kv[256:KEYS, 0:256].T
+    vt[:, 256:KEYS] = kv[256:KEYS, 256:512].T
+    nt_all[:, 256:KEYS] = nrm[256:KEYS, :].T
 
     def head(h):
         rows = slice(h * 64, (h + 1) * 64)
         heads = slice(h * 256, (h + 1) * 256)
-        s = nt(kv[:, 0:256], qm[heads, :]) * scale + bias[...]
-        top = jnp.max(s, axis=0, keepdims=True)
+        s = nt(kv[256:KEYS, 0:256], qm[heads, :]) * scale + bias[256:KEYS, :]
+        own_top = otop[h:h + 1, :]
+        top = jnp.maximum(own_top, jnp.max(s, axis=0, keepdims=True))
         e = jnp.exp(s - top)
-        p = e * (1.0 / jnp.sum(e, axis=0, keepdims=True))
-        w = p.astype(BF16)
-        wall[:, heads] = w
-        dp = nt(kv[:, 256:512], um[heads, :])
-        delta = jnp.sum(p * dp, axis=0, keepdims=True)
-        slope = (p * (dp - delta)).astype(BF16)
-        sall[:, heads] = slope
-        att[rows, :] = nn(vt[rows, :], w).astype(BF16)
-        dqt[rows, :] = nn(kt[rows, :], slope) * scale
+        shrink = jnp.exp(own_top - top)
+        inv = 1.0 / (osum[h:h + 1, :] * shrink + jnp.sum(e, axis=0, keepdims=True))
+        own_p = oexp[:, heads] * (shrink * inv)
+        p = e * inv
+        wall[0:256, heads] = own_p.astype(BF16)
+        wall[256:KEYS, heads] = p.astype(BF16)
+        dp = nt(kv[256:KEYS, 256:512], um[heads, :])
+        delta = odel[h:h + 1, :] * (shrink * inv) + jnp.sum(p * dp, axis=0, keepdims=True)
+        sall[0:256, heads] = (own_p * (odp[:, heads] - delta)).astype(BF16)
+        sall[256:KEYS, heads] = (p * (dp - delta)).astype(BF16)
+        att[rows, :] = nn(vt[rows, :], wall[:, heads]).astype(BF16)
+        dqt[rows, :] = nn(kt[rows, :], sall[:, heads]) * scale
 
     mark("head01")
     head(0)
     head(1)
-    mark("forward2")
-    ag_wait(opp, gx, 0)
-    ag_wait(opp, gx, 1)
-    for x in (far, right, left):
-        ag_send(opp, gx, (b, gy, x))
     mark("head23")
+    pl.semaphore_wait(heard.at[2], 3)
+    tell(heard.at[3], line)
     head(2)
     head(3)
 
+    mark("forward2")
+    pl.semaphore_wait(heard.at[3], 3)
+    drain(ag.at[0], r_ag.at[OPP])
+    for x in (far, right, left):
+        ag_send(opp, gx, (b, gy, x), REST)
     mark("finegrad")
-    nt_all[...] = nrm[...].T
     dq = dqt[...].T.astype(BF16)
     dk = (nn(sall[...], qm[...]) * scale).astype(BF16)
     dv = nn(wall[...], um[...]).astype(BF16)
@@ -292,20 +317,18 @@
         for i in range(2):
             fg[half, :, 256 * i:256 * (i + 1)] = parts[half][i]
             fgb[half, :, 256 * i:256 * (i + 1)] = parts[half][i].astype(BF16)
-    fcc = rcopy(fgb.at[1 - core], fgp, s_fc.at[0], r_fc.at[0], partner)
+    fcc = rcopy(fgb.at[1 - core], fgp, s_fc, r_fc, partner)
     fcc.start()
 
     mark("gsend")
     gsend[...] = (nt(dk[256:KEYS], wqkv[:, 256:512]) + nt(dv[256:KEYS], wqkv[:, 512:768])).astype(BF16)
-    ghalo = []
     for s in range(1, 9):
         dy, dx = FROM[s]
         o = BACK[s]
         c = rcopy(gsend.at[pl.ds(SEGMENTS[s][0] - 256, size(s))],
                   grecv.at[pl.ds(SEGMENTS[o][0] - 256, size(o))],
-                  s_g.at[s - 1], r_g.at[s - 1], toward((dy, dx)))
+                  s_g, r_g, toward((dy, dx)))
         c.start()
-        ghalo.append(c)
     dn[...] = (
         nt(dq, wqkv[:, 0:256]) + nt(dk[0:256], wqkv[:, 256:512]) + nt(dv[0:256], wqkv[:, 512:768])
     ).reshape(8, 32, 256)
@@ -313,34 +336,13 @@
     def spread(source, dest, ssem, rsem, me, device, each, n=16):
         def body(i, carry):
             p = lax.rem(me + i, n)
-            rcopy(source.at[p] if each else source, dest.at[me], ssem.at[i], rsem.at[me], device(p)).start()
+            rcopy(source.at[p] if each else source, dest.at[me], ssem, rsem, device(p)).start()
             return carry
         lax.fori_loop(1, n, body, 0)
 
-    def collect(source, dest, ssem, rsem, me, device, each, forward=None, n=16):
-        if forward is not None:
-            forward(me).start()
-
-        def body(i, carry):
-            p = lax.rem(me + i, n)
-            c = rcopy(source.at[p] if each else source, dest.at[p], ssem.at[i], rsem.at[p], device(p))
-            c.wait_recv()
-            if forward is not None:
-                forward(p).start()
-            c.wait_send()
-            return carry
-        lax.fori_loop(1, n, body, 0)
-
-    def to_partner(dest, ssem, rsem):
-        return lambda p: rcopy(dest.at[core, p], dest.at[core, p], ssem.at[p], rsem.at[p], partner)
-
-    def from_partner(dest, ssem, rsem, n=16):
-        def body(p, carry):
-            c = rcopy(dest.at[1 - core, p], dest.at[1 - core, p], ssem.at[p], rsem.at[p], partner)
-            c.wait_recv()
-            c.wait_send()
-            return carry
-        lax.fori_loop(0, n, body, 0)
+    def collect(dest, ssem, rsem, n=16):
+        drain(dest.at[pl.ds(0, n - 1)], rsem)
+        drain(dest.at[pl.ds(0, n - 1)], ssem)
 
     def total(dest, n=16):
         acc = dest[0].astype(F32)
@@ -351,16 +353,10 @@
     mark("fccwait")
     fcc.wait_recv()
     fxs[...] = (fg[core] + fgp[...].astype(F32)).astype(BF16).reshape(4, 64, 512)
-    fx = []
-    for i in (1, 3, 2):
-        x = lax.rem(gx + i, 4)
-        c = rcopy(fxs.at[x], fxr.at[i], s_fx.at[i], r_fx.at[i], (b, gy, x))
-        c.start()
-        fx.append(c)
+    spread(fxs, fxr, s_fx, r_fx, gx, along_x, True, n=4)
+
     mark("agwait")
-    for g in (gy, down, up, opp):
-        for x in (right, left, far):
-            ag_wait(g, x)
+    drain(ag.at[pl.ds(0, 12)], r_ag.at[REST])
     for c in loads[8:10]:
         c.wait()
     mark("coarse")
@@ -382,12 +378,7 @@
     ).astype(BF16)
     mark("rs")
     rs_send[...] = tn(cdt, cw[...]).astype(BF16).reshape(4, 4, 16, D_C)
-    rx = []
-    for i in (1, 3, 2):
-        x = lax.rem(gx + i, 4)
-        c = rcopy(rs_send.at[x], rsx.at[i], s_rx.at[i], r_rx.at[i], (b, gy, x))
-        c.start()
-        rx.append(c)
+    spread(rs_send, rsx, s_rx, r_rx, gx, along_x, True, n=4)
     mark("cgrad")
     cgq = nn(cdt, nall)
     cgo = nn(cot, call)
@@ -397,19 +388,17 @@
         cg[half, 192:256, :] = cgo[:, lanes]
         cgb[half, 0:192, :] = cgq[:, lanes].astype(BF16)
         cgb[half, 192:256, :] = cgo[:, lanes].astype(BF16)
-    cc = rcopy(cgb.at[1 - core], cgp, s_cc.at[0], r_cc.at[0], partner)
+    cc = rcopy(cgb.at[1 - core], cgp, s_cc, r_cc, partner)
     cc.start()
 
     mark("fxwait")
-    acc = fxs[gx].astype(F32)
-    for i, c in zip((1, 3, 2), fx):
-        c.wait_recv()
-        acc = acc + fxr[i].astype(F32)
+    collect(fxr, s_fx, r_fx, 4)
+    fxr[gx] = fxs[gx]
+    acc = total(fxr, 4)
     for j in range(2):
         fzs[4 * j:4 * j + 4] = acc[:, 256 * j:256 * (j + 1)].astype(BF16).reshape(4, 16, 256)
     fzr[zz] = fzs[zz]
     spread(fzs, fzr, s_fz, r_fz, zz, along_z, True, n=8)
-
     mark("ccwait")
     cc.wait_recv()
     c16[...] = (cg[core] + cgp[...].astype(F32)).astype(BF16).reshape(16, 16, 512)
@@ -417,26 +406,18 @@
     spread(c16, c16r, s_c16, r_c16, bz, batch, True)
 
     mark("fzwait")
-    collect(fzs, fzr, s_fz, r_fz, zz, along_z, True, n=8)
+    collect(fzr, s_fz, r_fz, 8)
     fyr[yy] = total(fzr, 8).astype(BF16)
     spread(fyr.at[yy], fyr, s_fy, r_fy, yy, along_y, False, n=8)
 
     mark("rsx")
-    acc = rs_send[gx].astype(F32)
-    for i, c in zip((1, 3, 2), rx):
-        c.wait_recv()
-        acc = acc + rsx[i].astype(F32)
-    rsz_send[...] = acc.astype(BF16)
-    rz = []
-    for i in (1, 3, 2):
-        g = lax.rem(gy + i, 4)
-        c = rcopy(rsz_send.at[g], rsz.at[i], s_rz.at[i], r_rz.at[i], (b, g, gx))
-        c.start()
-        rz.append(c)
+    collect(rsx, s_rx, r_rx, 4)
+    rsx[gx] = rs_send[gx]
+    rsz_send[...] = total(rsx, 4).astype(BF16)
+    spread(rsz_send, rsz, s_rz, r_rz, gy, lambda p: (b, p, gx), True, n=4)
 
     mark("ghalowait")
-    for c in ghalo:
-        c.wait_recv()
+    drain(grecv, r_g)
 
     def owed(s):
         first, rows, cols = SEGMENTS[s][:3]
@@ -453,24 +434,23 @@
     inv_f = lax.rsqrt(jnp.mean(xff * xff, axis=-1, keepdims=True) + eps)
     dxf[...] = norm_backward(xff, inv_f, ff[...], dn[...].reshape(256, 256))
 
+    mark("c16wait")
+    collect(c16r, s_c16, r_c16)
+    cmine = cfin.at[core, bz]
+    cmine[...] = total(c16r).astype(BF16)
+    spread(cmine, cfin.at[core], s_cag, r_cag.at[bz // 4], bz, batch, False)
+
     mark("fywait")
-    collect(fyr.at[yy], fyr, s_fy, r_fy, yy, along_y, False, n=8)
+    collect(fyr, s_fy, r_fy, 8)
     fcol = ffin.at[core, gx]
     fmine = fcol.at[zz]
     fmine[...] = total(fyr, 8).astype(BF16)
     spread(fmine, fcol, s_fzg, r_fzg, zz, along_z, False, n=8)
 
-    mark("c16wait")
-    collect(c16, c16r, s_c16, r_c16, bz, batch, True)
-    cmine = cfin.at[core, bz]
-    cmine[...] = total(c16r).astype(BF16)
-    spread(cmine, cfin.at[core], s_cag, r_cag, bz, batch, False)
-
     mark("rszwait")
-    dnc = rsz_send[gy].astype(F32)
-    for i, c in zip((1, 3, 2), rz):
-        c.wait_recv()
-        dnc = dnc + rsz[i].astype(F32)
+    collect(rsz, s_rz, r_rz, 4)
+    rsz[gy] = rsz_send[gy]
+    dnc = total(rsz, 4)
     xcf = xc[...]
     inv_c = lax.rsqrt(jnp.mean(xcf * xcf, axis=-1, keepdims=True) + eps)
     dxcv = norm_backward(xcf, inv_c, fc[...], dnc)
@@ -478,23 +458,37 @@
         dxc[r] = dxcv[4 * r:4 * r + 4]
 
     mark("fzgwait")
-    collect(fmine, fcol, s_fzg, r_fzg, zz, along_z, False, n=8)
-    spread(fcol, ffin.at[core], s_fxg, r_fxg, gx, lambda p: (b, gy, p), False, n=4)
+    collect(fcol, s_fzg, r_fzg, 8)
+
+    for i in (1, 3, 2):
+        rcopy(fcol, fcol, s_fxg, r_fxg.at[i], (b, gy, lax.rem(gx + i, 4))).start()
+    rcopy(fcol, fcol, s_ff, r_ff, partner).start()
 
     mark("cagwait")
-    collect(cmine, cfin.at[core], s_cag, r_cag, bz, batch, False, to_partner(cfin, s_cf, r_cf))
+    for k in (1, 2, 3, 4):
+        four = lax.rem(bz // 4 + k, 4)
+        drain(cfin.at[core, pl.ds(0, 4 if k < 4 else 3)], r_cag.at[four])
+        blocks = cfin.at[core, pl.ds(4 * four, 4)]
+        rcopy(blocks, blocks, s_cf, r_cf, partner).start()
+    mark("fxgwait")
+    for i in (1, 3, 2):
+        drain(fcol, r_fxg.at[i])
+        came = ffin.at[core, lax.rem(gx - i + 4, 4)]
+        rcopy(came, came, s_ff, r_ff, partner).start()
     mark("cfwait")
-    from_partner(cfin, s_cf, r_cf)
+    drain(cfin.at[0], r_cf)
+    drain(cfin.at[0], s_cf)
+    drain(cfin.at[0, pl.ds(0, 15)], s_cag)
     for half in range(2):
         lanes = slice(half * 512, (half + 1) * 512)
         done = cfin[half].reshape(256, 512)
         gcq[:, lanes] = done[0:192]
         gco[:, lanes] = done[192:256]
 
-    mark("fxgwait")
-    collect(fcol, ffin.at[core], s_fxg, r_fxg, gx, lambda p: (b, gy, p), False, to_partner(ffin, s_ff, r_ff), n=4)
     mark("ffwait")
-    from_partner(ffin, s_ff, r_ff, n=4)
+    drain(ffin.at[0], r_ff)
+    drain(ffin.at[0], s_ff)
+    drain(ffin.at[0, pl.ds(0, 3)], s_fxg)
     for x in range(4):
         rows = slice(64 * x, 64 * (x + 1))
         quarter = [ffin[half, x, 4 * j:4 * j + 4].reshape(64, 256) for half in range(2) for j in range(2)]
@@ -503,8 +497,11 @@
         gfo[rows, :] = quarter[3]
 
     mark("sendwait")
-    for c in sends + halo + ghalo + rx + rz + fx + [cc, fcc]:
-        c.wait_send()
+    drain(nrm.at[pl.ds(256, HALO)], s_h)
+    drain(grecv, s_g)
+    drain(ag.at[pl.ds(0, 15)], s_ag)
+    cc.wait_send()
+    fcc.wait_send()
     mark(None)
 
 
@@ -539,6 +536,7 @@
         V((KEYS, 256), F32), V((1024, 256), BF16), V((1024, 256), BF16),
         V((256, KEYS), BF16), V((256, KEYS), BF16), V((256, KEYS), BF16),
         V((KEYS, 1024), BF16), V((KEYS, 1024), BF16),
+        V((256, 1024), F32), V((256, 1024), F32), V((8, 256), F32), V((8, 256), F32), V((8, 256), F32),
         V((256, 256), BF16), V((256, 256), F32), V((8, 32, 256), F32),
         V((HALO, 256), BF16), V((HALO, 256), BF16),
         V((4, 4, 16, D_C), BF16), V((4, 4, 16, D_C), BF16), V((4, 16, D_C), BF16), V((4, 16, D_C), BF16),
@@ -547,11 +545,9 @@
         V((2, 256, 512), F32), V((2, 256, 512), BF16), V((256, 512), BF16),
         V((4, 64, 512), BF16), V((4, 64, 512), BF16), V((8, 16, 256), BF16), V((8, 16, 256), BF16),
         V((8, 16, 256), BF16), V((2, 4, 8, 16, 256), BF16),
-        dma((10,)), dma((16,)), dma((16, 2)), dma((8,)), dma((8,)), dma((8,)), dma((8,)),
-        dma((4,)), dma((4,)), dma((4,)), dma((4,)),
-        dma((2,)), dma((2,)), dma((16,)), dma((16,)), dma((16,)), dma((16,)), dma((16,)), dma((16,)),
-        dma((2,)), dma((2,)), dma((4,)), dma((4,)), dma((8,)), dma((8,)), dma((8,)), dma((8,)),
-        dma((8,)), dma((8,)), dma((4,)), dma((4,)), dma((4,)), dma((4,)),
+        pltpu.SemaphoreType.REGULAR((4,)), dma((10,)), dma, dma((4,)), dma, dma, dma, dma, dma, dma, dma, dma,
+        dma, dma, dma, dma, dma, dma((4,)), dma, dma,
+        dma, dma, dma, dma, dma, dma, dma, dma, dma, dma, dma, dma((4,)), dma, dma,
     ]
     results = pl.pallas_call(
         kernel,

time: 65.7 us -> 62.6 us (0.953)
  Pallas kernels: 64.3 us -> 61.1 us
    pallas_call x1, Pallas kernels: 63.2 us -> 60.1 us  [local(): pl.pallas_call(kernel, out_shape=outs, in_specs=[pl.BlockSpec(memory_spac...]
where the time goes in v4:
time: 62.6 us; the launch traced here: 62.4 us
  Pallas kernels  61.1 us (98%)
  between operations  1.29 us (2%)
    pallas_call x1, Pallas kernels, local(): pl.pallas_call(kernel, out_shape=outs, in_specs=[pl.BlockSpec(memory_spac...  60.1 us

profile of v4, /device:TPU:1, one launch (start us, length us, event | category | flops | bytes accessed | tf_op | source)
XLA Modules:
  0.0 62.4 jit_solution(15679226716966604398)
XLA Ops:
  1.3 60.1 %shard_map.154 = (bf16[256,256]{1,0:T(8,128)(2,1)S(1)}, bf16[4,4,1024]{2,1,0:T(4,128)(2,1)S(1)}, bf16[256,768]{1,0:T(8,128)(2,1)S(1)}, bf16[256,256]{1,0:T(8,128...) custom-call(s32[1]{0:T(128)S(6)} %copy.17.t_ref, bf16[256,256]{1,0:T(8,128)(2,1)} %bitcast.11, ...), custom_call_target="tpu_custom_call" | custom-call | tf_op jit(solution)/shard_map/pallas_call | solution.py:552
  61.4 1.1 %shard_map.155 = (bf16[256,256]{1,0:T(8,128)(2,1)}, bf16[4,4,1024]{2,1,0:T(4,128)(2,1)}, bf16[256,768]{1,0:T(8,128)(2,1)}, bf16[256,256]{1,0:T(8,128)(2,1)}, bf1...) custom-call(bf16[256,256]{1,0:T(8,128)(2,1)S(1)} %get-tuple-element.18.refs_0_, ...), custom_call_target="tpu_custom_call" | custom-call | tf_op jit(solution)/shard_map/pallas_call | solution.py:569

commit v5 on v4

--- a/solution.py
+++ b/solution.py
@@ -334,11 +334,13 @@
     ).reshape(8, 32, 256)
 
     def spread(source, dest, ssem, rsem, me, device, each, n=16):
-        def body(i, carry):
-            p = lax.rem(me + i, n)
-            rcopy(source.at[p] if each else source, dest.at[me], ssem, rsem, device(p)).start()
-            return carry
-        lax.fori_loop(1, n, body, 0)
+        ring = min(n, 8)
+        for other in range(n // ring - 1, -1, -1):
+            for o in sorted(range(ring), key=lambda o: -min(o, ring - o)):
+                if (other, o) == (0, 0):
+                    continue
+                p = lax.rem(me + o, ring) if n == ring else lax.rem(me // 8 + other, 2) * 8 + lax.rem(me + o, 8)
+                rcopy(source.at[p] if each else source, dest.at[me], ssem, rsem, device(p)).start()
 
     def collect(dest, ssem, rsem, n=16):
         drain(dest.at[pl.ds(0, n - 1)], rsem)
@@ -434,18 +436,18 @@
     inv_f = lax.rsqrt(jnp.mean(xff * xff, axis=-1, keepdims=True) + eps)
     dxf[...] = norm_backward(xff, inv_f, ff[...], dn[...].reshape(256, 256))
 
-    mark("c16wait")
-    collect(c16r, s_c16, r_c16)
-    cmine = cfin.at[core, bz]
-    cmine[...] = total(c16r).astype(BF16)
-    spread(cmine, cfin.at[core], s_cag, r_cag.at[bz // 4], bz, batch, False)
-
     mark("fywait")
     collect(fyr, s_fy, r_fy, 8)
     fcol = ffin.at[core, gx]
     fmine = fcol.at[zz]
     fmine[...] = total(fyr, 8).astype(BF16)
     spread(fmine, fcol, s_fzg, r_fzg, zz, along_z, False, n=8)
+
+    mark("c16wait")
+    collect(c16r, s_c16, r_c16)
+    cmine = cfin.at[core, bz]
+    cmine[...] = total(c16r).astype(BF16)
+    spread(cmine, cfin.at[core], s_cag, r_cag.at[bz // 4], bz, batch, False)
 
     mark("rszwait")
     collect(rsz, s_rz, r_rz, 4)

time: 62.6 us -> 61.1 us (0.976)
  Pallas kernels: 61.1 us -> 59.7 us
    pallas_call x1, Pallas kernels: 60.1 us -> 58.6 us  [local(): pl.pallas_call(kernel, out_shape=outs, in_specs=[pl.BlockSpec(memory_spac...]
where the time goes in v5:
time: 61.1 us; the launch traced here: 61 us
  Pallas kernels  59.7 us (98%)
  between operations  1.29 us (2%)
    pallas_call x1, Pallas kernels, local(): pl.pallas_call(kernel, out_shape=outs, in_specs=[pl.BlockSpec(memory_spac...  58.6 us

profile of v5, /device:TPU:1, one launch (start us, length us, event | category | flops | bytes accessed | tf_op | source)
XLA Modules:
  0.0 61.0 jit_solution(700461451985020080)
XLA Ops:
  1.3 58.6 %shard_map.154 = (bf16[256,256]{1,0:T(8,128)(2,1)S(1)}, bf16[4,4,1024]{2,1,0:T(4,128)(2,1)S(1)}, bf16[256,768]{1,0:T(8,128)(2,1)S(1)}, bf16[256,256]{1,0:T(8,128...) custom-call(s32[1]{0:T(128)S(6)} %copy.17.t_ref, bf16[256,256]{1,0:T(8,128)(2,1)} %bitcast.11, ...), custom_call_target="tpu_custom_call" | custom-call | tf_op jit(solution)/shard_map/pallas_call | solution.py:554
  59.9 1.1 %shard_map.155 = (bf16[256,256]{1,0:T(8,128)(2,1)}, bf16[4,4,1024]{2,1,0:T(4,128)(2,1)}, bf16[256,768]{1,0:T(8,128)(2,1)}, bf16[256,256]{1,0:T(8,128)(2,1)}, bf1...) custom-call(bf16[256,256]{1,0:T(8,128)(2,1)S(1)} %get-tuple-element.18.refs_0_, ...), custom_call_target="tpu_custom_call" | custom-call | tf_op jit(solution)/shard_map/pallas_call | solution.py:571

commit v6 on v5

--- a/solution.py
+++ b/solution.py
@@ -66,12 +66,11 @@
     pltpu.make_async_copy(ref, ref, sem).wait()
 
 
-def time_gain(gains, step_value):
-    channels = gains.shape[1]
+def time_wave(channels, step_value):
     place = lax.broadcasted_iota(jnp.int32, (8, channels), 1).astype(F32)
     frequency = jnp.exp(-log_span * place / channels)
     factor = jnp.cos(step_value * frequency)
-    return gains * (1.0 + 0.5 * factor[0:1])
+    return 1.0 + 0.5 * factor[0:1]
 
 
 def norm_backward(floats, inverse, factor, upstream):
@@ -146,10 +145,12 @@
 
     mark("norms")
     step_value = t_ref[0].astype(F32)
+    ff[...] = time_wave(D_F, step_value)
+    fc[...] = time_wave(D_C, step_value)
     for c in loads[0:3]:
         c.wait()
-    ff[...] = time_gain(gf[...], step_value)
-    fc[...] = time_gain(gc[...], step_value)
+    ff[...] = gf[...] * ff[...]
+    fc[...] = gc[...] * fc[...]
 
     xff = xf[...].astype(F32)
     inv_f = lax.rsqrt(jnp.mean(xff * xff, axis=-1, keepdims=True) + eps)
@@ -295,13 +296,10 @@
     head(0)
     head(1)
     mark("head23")
-    pl.semaphore_wait(heard.at[2], 3)
-    tell(heard.at[3], line)
     head(2)
     head(3)
 
     mark("forward2")
-    pl.semaphore_wait(heard.at[3], 3)
     drain(ag.at[0], r_ag.at[OPP])
     for x in (far, right, left):
         ag_send(opp, gx, (b, gy, x), REST)
@@ -357,6 +355,8 @@
     fxs[...] = (fg[core] + fgp[...].astype(F32)).astype(BF16).reshape(4, 64, 512)
     spread(fxs, fxr, s_fx, r_fx, gx, along_x, True, n=4)
 
+    pl.semaphore_wait(heard.at[2], 3)
+    tell(heard.at[3], line)
     mark("agwait")
     drain(ag.at[pl.ds(0, 12)], r_ag.at[REST])
     for c in loads[8:10]:
@@ -393,6 +393,7 @@
     cc = rcopy(cgb.at[1 - core], cgp, s_cc, r_cc, partner)
     cc.start()
 
+    pl.semaphore_wait(heard.at[3], 3)
     mark("fxwait")
     collect(fxr, s_fx, r_fx, 4)
     fxr[gx] = fxs[gx]

time: 61.1 us -> 61.9 us (1.013)
  Pallas kernels: 59.7 us -> 60.4 us
    pallas_call x1, Pallas kernels: 58.6 us -> 59.4 us  [local(): pl.pallas_call(kernel, out_shape=outs, in_specs=[pl.BlockSpec(memory_spac...]
where the time goes in v6:
time: 61.9 us; the launch traced here: 61.7 us
  Pallas kernels  60.4 us (98%)
  between operations  1.29 us (2%)
    pallas_call x1, Pallas kernels, local(): pl.pallas_call(kernel, out_shape=outs, in_specs=[pl.BlockSpec(memory_spac...  59.4 us

profile of v6, /device:TPU:1, one launch (start us, length us, event | category | flops | bytes accessed | tf_op | source)
XLA Modules:
  0.0 61.7 jit_solution(14936381802834402867)
XLA Ops:
  1.3 59.4 %shard_map.154 = (bf16[256,256]{1,0:T(8,128)(2,1)S(1)}, bf16[4,4,1024]{2,1,0:T(4,128)(2,1)S(1)}, bf16[256,768]{1,0:T(8,128)(2,1)S(1)}, bf16[256,256]{1,0:T(8,128...) custom-call(s32[1]{0:T(128)S(6)} %copy.17.t_ref, bf16[256,256]{1,0:T(8,128)(2,1)} %bitcast.11, ...), custom_call_target="tpu_custom_call" | custom-call | tf_op jit(solution)/shard_map/pallas_call | solution.py:555
  60.6 1.1 %shard_map.155 = (bf16[256,256]{1,0:T(8,128)(2,1)}, bf16[4,4,1024]{2,1,0:T(4,128)(2,1)}, bf16[256,768]{1,0:T(8,128)(2,1)}, bf16[256,256]{1,0:T(8,128)(2,1)}, bf1...) custom-call(bf16[256,256]{1,0:T(8,128)(2,1)S(1)} %get-tuple-element.18.refs_0_, ...), custom_call_target="tpu_custom_call" | custom-call | tf_op jit(solution)/shard_map/pallas_call | solution.py:572
